TPU v7x, 256 devices: a whole 4x4x8 slice. The times are simulated.
256 devices in a mesh: group: 4 (over y), member: 64 (over x, z, core).
Axes of the slice: x: 4, y: 4, z: 8, core: 2. Of those that a mesh axis runs over, the one named last changes fastest.
Arguments:
- embeddings: bfloat16 [8192, 39, 128], P(('group', 'member')), may hold values from -6 to 6
- cot_first: bfloat16 [8192, 100], P(('group', 'member')), may hold values from -6 to 6
- cot_second: bfloat16 [8192, 100], P(('group', 'member')), may hold values from -6 to 6
- cot_third: bfloat16 [8192, 100], P(('group', 'member')), may hold values from -6 to 6
- w_first: bfloat16 [100, 39, 39], replicated, may hold values from -0.15625 to 0.15625
- w_second: bfloat16 [100, 100, 39], replicated, may hold values from -0.09375 to 0.09375
- w_third: bfloat16 [100, 100, 39], replicated, may hold values from -0.09375 to 0.09375
- unique_ids: int32 [256, 768], P(('group', 'member')), may hold values from 0 to 1048575, as said below
- inverse: int32 [8192, 39], P(('group', 'member')), may hold values from 0 to 767, as said below
- table: float32 [1048576, 128], P(('group', 'member')), may hold values from -6 to 6
- accum: float32 [1048576], P(('group', 'member')), may hold values from 1 to 300
- next_ids: int32 [256, 1536], P(('group', 'member')), may hold values from 0 to 1048575, as said below
Outputs:
- new_table: float32 [1048576, 128], P(('group', 'member'))
- new_accum: float32 [1048576], P(('group', 'member'))
- returned: float32 [256, 1536, 128], P(('group', 'member'))
Inputs may be any that keep to these rules, and one draw needn't show every extreme that they name: `unique_ids`: row s lists 768 distinct table rows looked up by the samples of device s along group+member, ordered so that the owner r // 4096 never falls; at most 4 rows of one list have the same owner. `inverse`: lookup (n, f) names a position in row n // 32 of unique_ids; every position of a row is named by some lookup. `next_ids`: row s lists 1536 distinct table rows read by device s, ordered so that the owner r // 4096 never falls; at most 8 rows of one list have the same owner.
All inputs are finite; a program needn't handle non-finite values.
Results may differ from a plain program's by a relative error of at most 0.0007.
Values sent between devices are 32-bit elements; how exact they have to be, the bound alone decides.
A program may use at most 64 MiB of HBM per device.

v0:
```python
import jax
import jax.numpy as jnp
from jax import lax
from jax.sharding import PartitionSpec as P

CAP = 4
RCAP = 8


RATE = 0.5
EPS = 1e-08


def split_up(array, dim, peers):
    shape = array.shape
    parts = array.reshape(*shape[:dim], peers, shape[dim] // peers, *shape[dim + 1 :])
    return jnp.moveaxis(parts, dim, 0)


def laid_out(parts, dim):
    parts = jnp.moveaxis(parts, 0, dim)
    shape = parts.shape
    return parts.reshape(*shape[:dim], shape[dim] * shape[dim + 1], *shape[dim + 2 :])


def one_exchange(array, axis, axes, splits, concats):
    sizes = [lax.axis_size(a) for a in axes]
    parts = split_up(array, splits[0], sizes[0])
    parts = jnp.moveaxis(split_up(parts, splits[1] + 1, sizes[1]), 0, 1)
    inside = parts.shape[2:]
    parts = parts.reshape(-1, *inside)
    parts = lax.all_to_all(parts, axis, split_axis=0, concat_axis=0, tiled=True)
    parts = laid_out(parts.reshape(*sizes, *inside), concats[0] + 1)
    return laid_out(parts, concats[1])


def cin_block(inputs, first_cot, second_cot, third_cot, first_w, second_w, third_w):
    exact = lax.Precision.HIGHEST
    widened = inputs.astype(jnp.float32)
    pairs_one = (widened[:, :, None] * widened[:, None]).astype(jnp.bfloat16)
    layer_one = jnp.einsum(
        "hij,nijd->nhd", first_w, pairs_one, preferred_element_type=jnp.float32
    ).astype(jnp.bfloat16)
    one_wide = layer_one.astype(jnp.float32)
    pairs_two = (one_wide[:, :, None] * widened[:, None]).astype(jnp.bfloat16)
    layer_two = jnp.einsum(
        "hij,nijd->nhd", second_w, pairs_two, preferred_element_type=jnp.float32
    ).astype(jnp.bfloat16)
    two_wide = layer_two.astype(jnp.float32)
    top_map = jnp.einsum("hij,nh->nij", third_w, third_cot, preferred_element_type=jnp.float32)
    grad_two = jnp.einsum("nij,njd->nid", top_map, widened, precision=exact)
    grad_base = jnp.einsum("nij,nid->njd", top_map, two_wide, precision=exact)
    upper = (second_cot.astype(jnp.float32)[:, :, None] + grad_two).astype(jnp.bfloat16)
    middle = jnp.einsum("hij,nhd->nijd", second_w, upper, preferred_element_type=jnp.float32)
    grad_one = jnp.sum(middle * widened[:, None], axis=2)
    grad_base = grad_base + jnp.sum(middle * one_wide[:, :, None], axis=1)
    lower = (first_cot.astype(jnp.float32)[:, :, None] + grad_one).astype(jnp.bfloat16)
    bottom = jnp.einsum("hij,nhd->nijd", first_w, lower, preferred_element_type=jnp.float32)
    grad_base = (
        grad_base
        + jnp.sum(bottom * widened[:, None], axis=2)
        + jnp.sum(bottom * widened[:, :, None], axis=1)
    )
    return grad_base


def bucket(row_list, capacity, rows_dev):
    owner_of = row_list // rows_dev
    leading = jnp.searchsorted(owner_of, owner_of, side="left")
    within = jnp.arange(row_list.shape[0], dtype=jnp.int32) - leading
    return (owner_of * capacity + within, row_list - owner_of * rows_dev)


def local(
    embeddings,
    cot_first,
    cot_second,
    cot_third,
    w_first,
    w_second,
    w_third,
    unique_ids,
    inverse,
    table,
    accum,
    next_ids,
):
    samples, fields, width = embeddings.shape
    block_size = 4
    turns = samples // block_size

    def one_block(pieces):
        return cin_block(pieces[0], pieces[1], pieces[2], pieces[3], w_first, w_second, w_third)

    pieces = (
        embeddings.reshape(turns, block_size, fields, width),
        cot_first.reshape(turns, block_size, -1),
        cot_second.reshape(turns, block_size, -1),
        cot_third.reshape(turns, block_size, -1),
    )
    grads = lax.map(one_block, pieces).reshape(samples * fields, width)
    listed = unique_ids[0]
    merged = jax.ops.segment_sum(grads, inverse.reshape(-1), num_segments=listed.shape[0])
    groups = lax.axis_size("group")
    members = lax.axis_size("member")
    owners = groups * members
    rows_dev = table.shape[0]
    target, inside = bucket(listed, CAP, rows_dev)
    send_rows = (
        jnp.zeros((owners * CAP, width), jnp.float32)
        .at[target]
        .set(merged)
        .reshape(groups, members, CAP, width)
    )
    send_local = (
        jnp.full((owners * CAP,), rows_dev, jnp.int32)
        .at[target]
        .set(inside)
        .reshape(groups, members, CAP)
    )
    wanted = next_ids[0]
    ask_target, ask_inside = bucket(wanted, RCAP, rows_dev)
    ask_local = (
        jnp.full((owners * RCAP,), rows_dev, jnp.int32)
        .at[ask_target]
        .set(ask_inside)
        .reshape(groups, members, RCAP)
    )
    payload = (send_rows, send_local)
    received = (
        one_exchange(payload[0], ("group", "member"), ("group", "member"), (0, 1), (0, 1)),
        one_exchange(payload[1], ("group", "member"), ("group", "member"), (0, 1), (0, 1)),
    )
    got_rows = received[0]
    got_local = received[1]
    got_asks = one_exchange(ask_local, ("group", "member"), ("group", "member"), (0, 1), (0, 1))
    table_grad = jax.ops.segment_sum(
        got_rows.reshape(-1, width), got_local.reshape(-1), num_segments=rows_dev + 1
    )[:rows_dev]
    new_accum = accum + jnp.mean(table_grad * table_grad, axis=1)
    new_table = table - RATE * table_grad / (jnp.sqrt(new_accum) + EPS)[:, None]
    found = jnp.take(new_table, jnp.minimum(got_asks, rows_dev - 1), axis=0)
    found = jnp.where((got_asks < rows_dev)[..., None], found, 0.0)
    answers = one_exchange(found, ("member", "group"), ("member", "group"), (1, 0), (1, 0))
    returned = answers.reshape(-1, width)[ask_target]
    return (new_table, new_accum, returned[None])


def solution(mesh):
    in_specs = (
        P(("group", "member"), None, None),
        P(("group", "member"), None),
        P(("group", "member"), None),
        P(("group", "member"), None),
        P(),
        P(),
        P(),
        P(("group", "member"), None),
        P(("group", "member"), None),
        P(("group", "member"), None),
        P(("group", "member")),
        P(("group", "member"), None),
    )
    out_specs = (
        P(("group", "member"), None),
        P(("group", "member")),
        P(("group", "member"), None, None),
    )
    return jax.shard_map(local, mesh=mesh, in_specs=in_specs, out_specs=out_specs, check_vma=False)
```

profile of v0, /device:TPU:1, one launch (start us, length us, event | category | flops | bytes accessed | tf_op | source)
XLA Modules:
  0.0 340.8 jit_solution(9104948314629264559)
XLA Ops:
  1.4 32.8 %while.61 = (s32[]{:T(128)}, u32[768]{0:T(1024)S(1)}, u32[768]{0:T(1024)S(1)}, s32[768]{0:T(1024)S(1)}, s32[]{:T(128)}, /*index=5*/s32[]{:T(128)}, s32[]{}) while((s32[]{:T(128)}, u32[768]{0:T(1024)S(1)}, u32[768]{0:T(1024)S(1)}, s32[768]{0:T(1024)S(1)}, s32[]{:T(128)}, /*index=5*/s32[]{:T(128)}, s32[]{}) %tuple.101), condition=%wide.region_1.2_spmd.clone, body=%wide.region_0.1_spmd.clone.sunk | while | flops 14852 | bytes 57965 | solution.py:69
  1.4 3.2 gather_fusion
  4.7 3.2 gather_fusion
  8.0 3.2 gather_fusion
  11.3 3.2 gather_fusion
  14.6 3.2 gather_fusion
  34.2 3.4 scatter_custom_fusion
  38.4 15.6 %all-to-all-start = ((s32[256,1,1,4]{3,2,1,0:T(1,128)}), s32[256,1,1,4]{3,2,1,0:T(1,128)S(1)}, u32[]{:S(2)}, u32[]{:S(2)}) async-start(s32[256,1,1,4]{3,2,1,0:T(1,128)} %bitcast.20), calls=%async_computation | async-start | bytes 262144 | tf_op jit(solution)/shard_map/all_to_all | solution.py:32
  54.2 93.3 %while.62 = (s32[]{:T(128)}, u32[1536]{0:T(1024)S(1)}, u32[1536]{0:T(1024)S(1)}, s32[1536]{0:T(1024)S(1)}, s32[]{:T(128)}, /*index=5*/s32[]{:T(128)}, s32[]{}) while((s32[]{:T(128)}, u32[1536]{0:T(1024)S(1)}, u32[1536]{0:T(1024)S(1)}, s32[1536]{0:T(1024)S(1)}, s32[]{:T(128)}, /*index=5*/s32[]{:T(128)}, s32[]{}) %tuple.107), condition=%wide.region_14.15_spmd.clone, body=%wide.region_13.14_spmd.clone.sunk | while | flops 29700 | bytes 115821 | solution.py:69
  54.2 8.4 %gather_fusion.1 = s32[1536]{0:T(1024)S(1)} fusion(s32[1536]{0:T(1024)S(1)} %get-tuple-element.505, u32[2048]{0:T(1024)S(1)} %pad_clamp_fusion.6), kind=kCustom, calls=%fused_computation.1.clone.clone.1 | custom fusion | bytes 18432 | tf_op jit(solution)/shard_map/jit(searchsorted)/jit(_searchsorted_scan_impl)/vmap(jit(_searchsorted_scan_impl))/while/body/eval_jaxpr/gather | solution.py:69
  62.7 8.4 %gather_fusion.1 = s32[1536]{0:T(1024)S(1)} fusion(s32[1536]{0:T(1024)S(1)} %get-tuple-element.505, u32[2048]{0:T(1024)S(1)} %pad_clamp_fusion.6), kind=kCustom, calls=%fused_computation.1.clone.clone.1 | custom fusion | bytes 18432 | tf_op jit(solution)/shard_map/jit(searchsorted)/jit(_searchsorted_scan_impl)/vmap(jit(_searchsorted_scan_impl))/while/body/eval_jaxpr/gather | solution.py:69
  71.2 8.4 %gather_fusion.1 = s32[1536]{0:T(1024)S(1)} fusion(s32[1536]{0:T(1024)S(1)} %get-tuple-element.505, u32[2048]{0:T(1024)S(1)} %pad_clamp_fusion.6), kind=kCustom, calls=%fused_computation.1.clone.clone.1 | custom fusion | bytes 18432 | tf_op jit(solution)/shard_map/jit(searchsorted)/jit(_searchsorted_scan_impl)/vmap(jit(_searchsorted_scan_impl))/while/body/eval_jaxpr/gather | solution.py:69
  79.7 8.4 %gather_fusion.1 = s32[1536]{0:T(1024)S(1)} fusion(s32[1536]{0:T(1024)S(1)} %get-tuple-element.505, u32[2048]{0:T(1024)S(1)} %pad_clamp_fusion.6), kind=kCustom, calls=%fused_computation.1.clone.clone.1 | custom fusion | bytes 18432 | tf_op jit(solution)/shard_map/jit(searchsorted)/jit(_searchsorted_scan_impl)/vmap(jit(_searchsorted_scan_impl))/while/body/eval_jaxpr/gather | solution.py:69
  88.1 8.4 %gather_fusion.1 = s32[1536]{0:T(1024)S(1)} fusion(s32[1536]{0:T(1024)S(1)} %get-tuple-element.505, u32[2048]{0:T(1024)S(1)} %pad_clamp_fusion.6), kind=kCustom, calls=%fused_computation.1.clone.clone.1 | custom fusion | bytes 18432 | tf_op jit(solution)/shard_map/jit(searchsorted)/jit(_searchsorted_scan_impl)/vmap(jit(_searchsorted_scan_impl))/while/body/eval_jaxpr/gather | solution.py:69
  96.6 8.4 %gather_fusion.1 = s32[1536]{0:T(1024)S(1)} fusion(s32[1536]{0:T(1024)S(1)} %get-tuple-element.505, u32[2048]{0:T(1024)S(1)} %pad_clamp_fusion.6), kind=kCustom, calls=%fused_computation.1.clone.clone.1 | custom fusion | bytes 18432 | tf_op jit(solution)/shard_map/jit(searchsorted)/jit(_searchsorted_scan_impl)/vmap(jit(_searchsorted_scan_impl))/while/body/eval_jaxpr/gather | solution.py:69
  105.1 8.4 %gather_fusion.1 = s32[1536]{0:T(1024)S(1)} fusion(s32[1536]{0:T(1024)S(1)} %get-tuple-element.505, u32[2048]{0:T(1024)S(1)} %pad_clamp_fusion.6), kind=kCustom, calls=%fused_computation.1.clone.clone.1 | custom fusion | bytes 18432 | tf_op jit(solution)/shard_map/jit(searchsorted)/jit(_searchsorted_scan_impl)/vmap(jit(_searchsorted_scan_impl))/while/body/eval_jaxpr/gather | solution.py:69
  113.6 8.4 %gather_fusion.1 = s32[1536]{0:T(1024)S(1)} fusion(s32[1536]{0:T(1024)S(1)} %get-tuple-element.505, u32[2048]{0:T(1024)S(1)} %pad_clamp_fusion.6), kind=kCustom, calls=%fused_computation.1.clone.clone.1 | custom fusion | bytes 18432 | tf_op jit(solution)/shard_map/jit(searchsorted)/jit(_searchsorted_scan_impl)/vmap(jit(_searchsorted_scan_impl))/while/body/eval_jaxpr/gather | solution.py:69
  122.1 8.4 %gather_fusion.1 = s32[1536]{0:T(1024)S(1)} fusion(s32[1536]{0:T(1024)S(1)} %get-tuple-element.505, u32[2048]{0:T(1024)S(1)} %pad_clamp_fusion.6), kind=kCustom, calls=%fused_computation.1.clone.clone.1 | custom fusion | bytes 18432 | tf_op jit(solution)/shard_map/jit(searchsorted)/jit(_searchsorted_scan_impl)/vmap(jit(_searchsorted_scan_impl))/while/body/eval_jaxpr/gather | solution.py:69
  130.6 8.4 %gather_fusion.1 = s32[1536]{0:T(1024)S(1)} fusion(s32[1536]{0:T(1024)S(1)} %get-tuple-element.505, u32[2048]{0:T(1024)S(1)} %pad_clamp_fusion.6), kind=kCustom, calls=%fused_computation.1.clone.clone.1 | custom fusion | bytes 18432 | tf_op jit(solution)/shard_map/jit(searchsorted)/jit(_searchsorted_scan_impl)/vmap(jit(_searchsorted_scan_impl))/while/body/eval_jaxpr/gather | solution.py:69
  139.0 8.4 %gather_fusion.1 = s32[1536]{0:T(1024)S(1)} fusion(s32[1536]{0:T(1024)S(1)} %get-tuple-element.505, u32[2048]{0:T(1024)S(1)} %pad_clamp_fusion.6), kind=kCustom, calls=%fused_computation.1.clone.clone.1 | custom fusion | bytes 18432 | tf_op jit(solution)/shard_map/jit(searchsorted)/jit(_searchsorted_scan_impl)/vmap(jit(_searchsorted_scan_impl))/while/body/eval_jaxpr/gather | solution.py:69
  151.1 6.2 %scatter_custom_fusion.4 = s32[2048]{0:T(1024)S(1)} fusion(s32[1536]{0:T(1024)S(1)} %get-tuple-element.309, s32[1536]{0:T(1024)S(1)} %get-tuple-element.308, s32[]{:T(128)} %constant.132.clone.1), kind=kCustom, calls=%fused_computation.105 | custom fusion | bytes 8196 | tf_op jit(solution)/shard_map/scatter | solution.py:126
  158.0 13.7 %all-to-all-start.2 = ((s32[256,1,1,8]{3,2,1,0:T(1,128)}), s32[256,1,1,8]{3,2,1,0:T(1,128)S(1)}, u32[]{:S(2)}, u32[]{:S(2)}) async-start(s32[256,1,1,8]{3,2,1,0:T(1,128)} %bitcast.35), calls=%async_computation.2 | async-start | bytes 262144 | tf_op jit(solution)/shard_map/all_to_all | solution.py:32
  171.8 60.1 %while.60 = (s32[]{:T(128)}, f32[8,4,39,128]{3,2,1,0:T(8,128)S(1)}, bf16[8,4,100]{2,1,0:T(4,128)(2,1)}, bf16[100,100,39]{1,0,2:T(8,128)(2,1)S(1)}, bf16[8,4,39,1...) while((s32[]{:T(128)}, f32[8,4,39,128]{3,2,1,0:T(8,128)S(1)}, ...), condition=%wide.region_8.9_spmd, body=%wide.region_3.8_spmd.sunk | while | flops 1178245248 | bytes 6882221 | solution.py:101
  232.0 9.0 %scatter_custom_fusion.1 = f32[768,128]{1,0:T(8,128)S(1)} fusion(s32[1248]{0:T(1024)S(1)} %reshape.179, f32[1248,128]{1,0:T(8,128)S(1)} %reshape.181, f32[]{:T(128)} %constant.131.clone.1), kind=kCustom, calls=%fused_computation.81 | custom fusion | flops 159744 | bytes 393220 | tf_op jit(solution)/shard_map/scatter-add | solution.py:103
  241.0 4.9 %scatter_custom_fusion.2 = f32[1024,128]{1,0:T(8,128)} fusion(s32[768]{0:T(1024)S(1)} %get-tuple-element.311, f32[768,128]{1,0:T(8,128)S(1)} %scatter_custom_fusion.1, f32[]{:T(128)} %constant.131.clone.1), kind=kCustom, calls=%fused_computation.79 | custom fusion | bytes 524292 | tf_op jit(solution)/shard_map/scatter | solution.py:112
  246.1 13.7 %all-to-all-start.1 = ((f32[256,1,1,4,128]{4,3,2,1,0:T(4,128)}), f32[256,1,1,4,128]{4,3,2,1,0:T(4,128)S(1)}, u32[]{:S(2)}, u32[]{:S(2)}) async-start(f32[256,1,1,4,128]{4,3,2,1,0:T(4,128)} %bitcast.29), calls=%async_computation.1 | async-start | bytes 1048576 | tf_op jit(solution)/shard_map/all_to_all | solution.py:32
  260.5 20.7 %all-to-all-done.1 = f32[256,1,1,4,128]{4,3,2,1,0:T(4,128)S(1)} async-done(((f32[256,1,1,4,128]{4,3,2,1,0:T(4,128)}), f32[256,1,1,4,128]{4,3,2,1,0:T(4,128)S(1)}, u32[]{:S(2)}, u32[]{:S(2)}) %all-to-all-start.1) | async-done | bytes 524320 | tf_op jit(solution)/shard_map/all_to_all | solution.py:32
  281.2 6.5 %scatter_custom_fusion.3 = f32[4097,128]{1,0:T(8,128)S(1)} fusion(s32[1024]{0:T(1024)S(1)} %reshape.195, f32[1024,128]{1,0:T(8,128)S(1)} %bitcast.190, f32[]{:T(128)} %constant.131.clone.1), kind=kCustom, calls=%fused_computation.73 | custom fusion | flops 131072 | bytes 2097668 | tf_op jit(solution)/shard_map/scatter-add | solution.py:137
  292.1 5.5 %gather_fusion.2 = f32[2048,128]{1,0:T(8,128)S(1)} fusion(f32[4096,128]{1,0:T(8,128)S(1)} %divide_subtract_fusion, s32[2048]{0:T(1024)S(1)} %broadcast_clamp_fusion), kind=kCustom, calls=%fused_computation.2 | custom fusion | bytes 2105344 | tf_op jit(solution)/shard_map/jit(_take)/gather | solution.py:142
  299.1 5.4 %all-to-all-start.3 = ((f32[256,1,1,8,128]{4,3,2,1,0:T(8,128)}), f32[256,1,1,8,128]{4,3,2,1,0:T(8,128)S(1)}, u32[]{:S(2)}, u32[]{:S(2)}) async-start(f32[256,1,1,8,128]{4,3,2,1,0:T(8,128)} %bitcast.54), calls=%async_computation.3 | async-start | bytes 2097152 | tf_op jit(solution)/shard_map/all_to_all | solution.py:32
  304.5 32.5 %all-to-all-done.3 = f32[256,1,1,8,128]{4,3,2,1,0:T(8,128)S(1)} async-done(((f32[256,1,1,8,128]{4,3,2,1,0:T(8,128)}), f32[256,1,1,8,128]{4,3,2,1,0:T(8,128)S(1)}, u32[]{:S(2)}, u32[]{:S(2)}) %all-to-all-start.3) | async-done | bytes 1048608 | tf_op jit(solution)/shard_map/all_to_all | solution.py:32
  337.1 3.7 %gather_fusion.3 = f32[1536,128]{1,0:T(8,128)} fusion(f32[2048,128]{1,0:T(8,128)S(1)} %bitcast.183, s32[2048]{0:T(1024)S(1)} %pad_clamp_fusion.2), kind=kCustom, calls=%fused_computation.3 | custom fusion | bytes 1579008 | tf_op jit(solution)/shard_map/gather | solution.py:145
  (251 shorter events, 88.8 us)
Async XLA Ops:
  1.4 52.7 %copy-start.7 = (s32[1,1536]{1,0:T(1,128)S(1)}, s32[1,1536]{1,0:T(1,128)}, u32[]{:S(2)}) copy-start(s32[1,1536]{1,0:T(1,128)} %param.29) | copy-start | bytes 18436
  38.4 119.6 %all-to-all-start = ((s32[256,1,1,4]{3,2,1,0:T(1,128)}), s32[256,1,1,4]{3,2,1,0:T(1,128)S(1)}, u32[]{:S(2)}, u32[]{:S(2)}) async-start(s32[256,1,1,4]{3,2,1,0:T(1,128)} %bitcast.20), calls=%async_computation | async-start | bytes 262144 | tf_op jit(solution)/shard_map/all_to_all | solution.py:32
  54.1 93.4 %copy-start.3 = (bf16[100,100,39]{1,2,0:T(8,128)(2,1)S(1)}, bf16[100,100,39]{1,2,0:T(8,128)(2,1)}, u32[]{:S(2)}) copy-start(bf16[100,100,39]{1,2,0:T(8,128)(2,1)} %param.24) | copy-start | bytes 2340004
  147.5 1.0 copy-start.4
  158.0 88.1 %all-to-all-start.2 = ((s32[256,1,1,8]{3,2,1,0:T(1,128)}), s32[256,1,1,8]{3,2,1,0:T(1,128)S(1)}, u32[]{:S(2)}, u32[]{:S(2)}) async-start(s32[256,1,1,8]{3,2,1,0:T(1,128)} %bitcast.35), calls=%async_computation.2 | async-start | bytes 262144 | tf_op jit(solution)/shard_map/all_to_all | solution.py:32
  171.7 60.1 %copy-start.5 = (s32[32,39]{1,0:T(8,128)S(1)}, s32[32,39]{1,0:T(8,128)}, u32[]{:S(2)}) copy-start(s32[32,39]{1,0:T(8,128)} %param.26) | copy-start | bytes 14980
  175.3 1.9 copy-start.8
  182.8 1.8 copy-start.8
  190.3 1.8 copy-start.8
  197.9 1.8 copy-start.8
  205.4 1.8 copy-start.8
  212.9 1.8 copy-start.8
  220.4 1.8 copy-start.8
  227.9 1.8 copy-start.8
  246.1 35.1 %all-to-all-start.1 = ((f32[256,1,1,4,128]{4,3,2,1,0:T(4,128)}), f32[256,1,1,4,128]{4,3,2,1,0:T(4,128)S(1)}, u32[]{:S(2)}, u32[]{:S(2)}) async-start(f32[256,1,1,4,128]{4,3,2,1,0:T(4,128)} %bitcast.29), calls=%async_computation.1 | async-start | bytes 1048576 | tf_op jit(solution)/shard_map/all_to_all | solution.py:32
  281.2 7.1 %copy-start.6 = (f32[4096]{0:T(1024)S(1)}, f32[4096]{0:T(1024)}, u32[]{:S(2)}) copy-start(f32[4096]{0:T(1024)} %param.28) | copy-start | bytes 49156
  287.7 1.4 copy-start.1
  287.7 2.4 copy-start.2
  292.1 5.5 %copy-start = (f32[4096,128]{1,0:T(8,128)}, f32[4096,128]{1,0:T(8,128)S(1)}, u32[]{:S(2)}) copy-start(f32[4096,128]{1,0:T(8,128)S(1)} %divide_subtract_fusion) | copy-start | bytes 6291460
  299.1 38.0 %all-to-all-start.3 = ((f32[256,1,1,8,128]{4,3,2,1,0:T(8,128)}), f32[256,1,1,8,128]{4,3,2,1,0:T(8,128)S(1)}, u32[]{:S(2)}, u32[]{:S(2)}) async-start(f32[256,1,1,8,128]{4,3,2,1,0:T(8,128)} %bitcast.54), calls=%async_computation.3 | async-start | bytes 2097152 | tf_op jit(solution)/shard_map/all_to_all | solution.py:32
where the time goes:
time: 342 us; the launch traced here: 341 us
  local copies, waits for them, and re-layouts  155 us (45%)
  matrix products  53.6 us (16%)
  waiting for transfers between devices  53.3 us (16%)
  starting transfers between devices  48.5 us (14%)
  other arithmetic  27.6 us (8%)
    gather x21, local copies, waits for them, and re-layouts, bucket(): leading = jnp.searchsorted(owner_of, owner_of, side='left')  124 us
    all_to_all x4, waiting for transfers between devices, one_exchange(): parts = lax.all_to_all(parts, axis, split_axis=0, concat_axis=0, tiled=True)  53.3 us
    all_to_all x4, starting transfers between devices, one_exchange(): parts = lax.all_to_all(parts, axis, split_axis=0, concat_axis=0, tiled=True)  48.5 us
    dot_general x8, matrix products, cin_block(): jnp.einsum('hij,nhd->nijd', second_w, upper, preferred_element_type=jnp.f...  14.6 us
    dot_general x8, matrix products, cin_block(): jnp.einsum('hij,nijd->nhd', first_w, pairs_one, preferred_element_type=jn...  11.9 us
    scatter-add x1, other arithmetic, local(): jax.ops.segment_sum(grads, inverse.reshape(-1), num_segments=listed.shape...  9 us
    dot_general x8, matrix products, cin_block(): jnp.einsum('hij,nh->nij', third_w, third_cot, preferred_element_type=jnp....  7.58 us
    dot_general x8, matrix products, cin_block(): jnp.einsum('hij,nhd->nijd', first_w, lower, preferred_element_type=jnp.fl...  7.57 us
  transfers between devices with their start and end apart: 4, of which 2 were waited for; matrix products, arithmetic and copies ran while one was open for 52% of the time, Pallas kernels for 0%

commit v1 on v0

v1 whole, which is shorter than its diff:
```python
import jax
import jax.numpy as jnp
from jax import lax
from jax.experimental import pallas as pl
from jax.experimental.pallas import tpu as pltpu
from jax.sharding import PartitionSpec as P

CAP = 4
RCAP = 8
RATE = 0.5
EPS = 1e-08

BF = jnp.bfloat16
F32 = jnp.float32


def halves(x):
    hi = x.astype(BF)
    return hi, (x - hi.astype(F32)).astype(BF)


def dot(a, b):
    return jnp.dot(a, b, preferred_element_type=F32)


FP = 48
FQ = 40
HP = 112
HQ = 104
KP = 128
JC = 3


def cin_kernel(
    fields,
    e_ref, c1_ref, c2_ref, thi_ref, tlo_ref, uhi_ref, ulo_ref,
    w1f_ref, w2f_ref, w2b_ref, w1b_ref,
    out_ref,
    ef, p1, p2, l1f, mid, bot, part, l2s,
):
    lanes = 256
    e = jnp.concatenate([e_ref[0], e_ref[1]], axis=1)
    ef[...] = e.astype(F32)
    e3 = e.reshape(FP // 16, 16, lanes)

    def row16(i):
        return jnp.broadcast_to(ef[i : i + 1, :], (16, lanes)).astype(BF)

    uppers = []
    for s in range(2):
        grad_two = dot(thi_ref[s], e_ref[s]) + dot(tlo_ref[s], e_ref[s])
        uppers.append((c2_ref[0, :, s : s + 1] + grad_two).astype(BF))
    upper = jnp.concatenate(uppers, axis=1)
    upper = jnp.concatenate([upper, jnp.zeros((KP - HP, lanes), BF)], axis=0)

    for i in range(fields):
        p1[i * FP : (i + 1) * FP, :] = (e3 * row16(i)[None]).reshape(FP, lanes)
    l1 = dot(w1f_ref[...], p1[...]).astype(BF)
    l1f[...] = l1.astype(F32)
    l3 = l1.reshape(HP // 16, 16, lanes)

    acc = [jnp.zeros((HQ // 8, 8, 128), F32) for _ in range(2)]
    done = 0
    l2 = None
    for c in range(fields // JC):
        mid[c % 2] = dot(w2b_ref[c * JC * HP : (c + 1) * JC * HP, :], upper)
        for k in range(JC):
            j = c * JC + k
            p2[j * HP : (j + 1) * HP, :] = (l3 * row16(j)[None]).reshape(HP, lanes)
        ready = (c + 1) * JC * HP
        if c + 1 < fields // JC:
            ready = ready // 512 * 512
        if ready > done:
            piece = dot(w2f_ref[:, done:ready], p2[done:ready, :])
            if done:
                piece = piece + l2s[...]
            l2s[...] = piece
            done = ready
        for s in range(2):
            ls = slice(s * 128, (s + 1) * 128)
            one = l1f[:HQ, ls].reshape(HQ // 8, 8, 128)
            for k in range(JC):
                j = c * JC + k
                m = mid[c % 2, k * HP : k * HP + HQ, ls].reshape(HQ // 8, 8, 128)
                b = jnp.broadcast_to(ef[j : j + 1, ls], (8, 128))
                acc[s] = acc[s] + m * b[None]
                part[j, :, ls] = jnp.sum(m * one, axis=0)
    l2 = l2s[...].astype(BF)
    bases = [
        dot(uhi_ref[s], l2[:, s * 128 : (s + 1) * 128]) + dot(ulo_ref[s], l2[:, s * 128 : (s + 1) * 128])
        for s in range(2)
    ]
    lower = jnp.concatenate(
        [(c1_ref[0, :HQ, s : s + 1] + acc[s].reshape(HQ, 128)).astype(F32) for s in range(2)], axis=1
    )
    lower = jnp.concatenate([lower, jnp.zeros((KP - HQ, lanes), F32)], axis=0).astype(BF)
    lower = jnp.concatenate([lower, lower], axis=0)
    for c in range(FQ // 8):
        buf = c % 2
        bot[buf] = dot(w1b_ref[c * 8 * FQ : (c + 1) * 8 * FQ, :], lower)
        for s in range(2):
            ls = slice(s * 128, (s + 1) * 128)
            es = ef[:FQ, ls].reshape(FQ // 8, 8, 128)
            for k in range(8):
                j = c * 8 + k
                m = bot[buf, k * FQ : (k + 1) * FQ, ls].reshape(FQ // 8, 8, 128)
                t = jnp.sum(m * es, axis=0)
                if j < fields:
                    t = t + part[j, :, ls]
                part[j, :, ls] = t
    for s in range(2):
        ls = slice(s * 128, (s + 1) * 128)
        out_ref[s] = jnp.sum(part[:, :, ls], axis=1) + bases[s][:FQ]


def cin(embeddings, cot_first, cot_second, cot_third, w_first, w_second, w_third):
    samples, fields, width = embeddings.shape
    maps = cot_first.shape[1]
    e = jnp.pad(embeddings, ((0, 0), (0, FP - fields), (0, 0)))

    def columns(cot):
        cot = jnp.pad(cot.astype(F32), ((0, 0), (0, HP - maps)))
        return jnp.transpose(cot.reshape(samples // 2, 2, HP), (0, 2, 1))

    top = jnp.einsum("hij,nh->nij", w_third, cot_third, preferred_element_type=F32)
    top = jnp.pad(top, ((0, 0), (0, HP - maps), (0, FP - fields)))
    thi, tlo = halves(top)
    uhi, ulo = jnp.swapaxes(thi, 1, 2), jnp.swapaxes(tlo, 1, 2)

    w2b = jnp.pad(jnp.transpose(w_second, (2, 1, 0)), ((0, 0), (0, HP - maps), (0, KP - maps)))
    w2b = w2b.reshape(fields * HP, KP)
    w2f = w2b.T[:HP]
    w1t = jnp.pad(jnp.transpose(w_first, (2, 1, 0)), ((0, 0), (0, FP - fields), (0, HP - maps)))
    w1f = w1t.reshape(fields * FP, HP).T
    both = w_first.astype(F32)
    both = both + jnp.swapaxes(both, 1, 2)
    both = jnp.pad(jnp.transpose(both, (2, 1, 0)), ((0, FQ - fields), (0, FQ - fields), (0, KP - maps)))
    w1b = jnp.concatenate(halves(both), axis=2).reshape(FQ * FQ, 2 * KP)

    def per(*shape):
        return pl.BlockSpec(shape, lambda g: (g,) + (0,) * (len(shape) - 1))

    def whole(x):
        return pl.BlockSpec(x.shape, lambda g: (0,) * x.ndim, pipeline_mode=pl.Buffered(1))

    def kernel(*refs):
        cin_kernel(fields, *refs)

    return pl.pallas_call(
        kernel,
        grid=(samples // 2,),
        in_specs=[
            per(2, FP, width), per(1, HP, 2), per(1, HP, 2),
            per(2, HP, FP), per(2, HP, FP), per(2, FP, HP), per(2, FP, HP),
            whole(w1f), whole(w2f), whole(w2b), whole(w1b),
        ],
        out_specs=per(2, FQ, width),
        out_shape=jax.ShapeDtypeStruct((samples, FQ, width), F32),
        scratch_shapes=[
            pltpu.VMEM((FP, 256), F32),
            pltpu.VMEM((fields * FP, 256), BF),
            pltpu.VMEM((fields * HP, 256), BF),
            pltpu.VMEM((HP, 256), F32),
            pltpu.VMEM((2, JC * HP, 256), F32),
            pltpu.VMEM((2, 8 * FQ, 256), F32),
            pltpu.VMEM((FQ, 8, 256), F32),
            pltpu.VMEM((HP, 256), F32),
        ],
        compiler_params=pltpu.CompilerParams(vmem_limit_bytes=48 << 20),
        name="cin",
    )(e, columns(cot_first), columns(cot_second), thi, tlo, uhi, ulo, w1f, w2f, w2b, w1b)


def ranks(row_list, capacity, rows_dev):
    owner = row_list // rows_dev
    within = jnp.zeros_like(owner)
    for k in range(1, capacity):
        earlier = jnp.concatenate([jnp.full((k,), -1, jnp.int32), owner[:-k]])
        within = within + (earlier == owner).astype(jnp.int32)
    return owner, within, row_list - owner * rows_dev


def by_owner(owner, within, inside, owners, capacity):
    hot = (jnp.arange(owners, dtype=jnp.int32)[:, None] == owner[None, :]).astype(BF)
    places = jnp.arange(capacity, dtype=jnp.int32)[None, :]
    value = jnp.where(within[:, None] == places, inside[:, None] + 1, 0)
    value = jnp.concatenate([value // 64, value % 64], axis=1).astype(BF)
    found = jnp.dot(hot, value, preferred_element_type=F32)
    return (found[:, :capacity] * 64 + found[:, capacity:]).astype(jnp.int32) - 1


def merge_kernel(inv_ref, target_ref, grads_ref, out_ref, hot, pair):
    count, listed = pair.shape[0], target_ref.shape[1]
    pair[...] = jnp.concatenate(halves(grads_ref[...]), axis=1)
    merged = []
    rows = 256
    for b in range(listed // rows):
        place = lax.broadcasted_iota(jnp.int32, (rows, count), 0) + b * rows
        hot[...] = jnp.where(place == inv_ref[...], 1.0, 0.0).astype(BF)
        m = dot(hot[...], pair[...])
        merged.append(m[:, :128] + m[:, 128:])
    merged = jnp.concatenate(halves(jnp.concatenate(merged, axis=0)), axis=1)
    for b in range(out_ref.shape[0] // rows):
        place = lax.broadcasted_iota(jnp.int32, (rows, listed), 0) + b * rows
        m = dot(jnp.where(place == target_ref[...], 1.0, 0.0).astype(BF), merged)
        out_ref[b * rows : (b + 1) * rows, :] = m[:, :128] + m[:, 128:]


def merge(grads, inverse, target, slots):
    samples, padded, width = grads.shape
    inv = jnp.pad(inverse, ((0, 0), (0, padded - inverse.shape[1])), constant_values=-1).reshape(1, -1)
    count = samples * padded
    return pl.pallas_call(
        merge_kernel,
        out_shape=jax.ShapeDtypeStruct((slots, width), F32),
        scratch_shapes=[pltpu.VMEM((256, count), BF), pltpu.VMEM((count, 2 * width), BF)],
        compiler_params=pltpu.CompilerParams(vmem_limit_bytes=32 << 20),
        name="merge",
    )(inv, target.reshape(1, -1), grads.reshape(count, width))


def update_kernel(loc_ref, rows_ref, table_ref, accum_ref, ask_ref, nt_ref, na_ref, found_ref, hot, pair, grad):
    pair[...] = jnp.concatenate(halves(rows_ref[...]), axis=1)
    got = pair.shape[0]
    lane = lax.broadcasted_iota(jnp.int32, (128, 128), 1)
    for b in range(table_ref.shape[0] // 1024):
        for r in range(8):
            place = lax.broadcasted_iota(jnp.int32, (128, got), 0) + (b * 1024 + r * 128)
            hot[r * 128 : (r + 1) * 128, :] = jnp.where(place == loc_ref[...], 1.0, 0.0).astype(BF)
        g = dot(hot[...], pair[...])
        grad[...] = g[:, :128] + g[:, 128:]
        means = jnp.zeros((128, 128), F32)
        for r in range(8):
            part = grad[r * 128 : (r + 1) * 128, :]
            means = jnp.where(lane == r, jnp.mean(part * part, axis=1, keepdims=True), means)
        na = accum_ref[8 * b : 8 * b + 8, :] + means.T[:8]
        na_ref[8 * b : 8 * b + 8, :] = na
        scale = RATE / (jnp.sqrt(na) + EPS)
        scale = jnp.concatenate([scale, jnp.zeros((120, 128), F32)], axis=0).T
        for r in range(8):
            at = slice(b * 1024 + r * 128, b * 1024 + (r + 1) * 128)
            nt_ref[at, :] = table_ref[at, :] - grad[r * 128 : (r + 1) * 128, :] * scale[:, r : r + 1]

    def gather(k, carry):
        for t in range(8):
            found_ref[pl.ds(k * 8 + t, 1), :] = nt_ref[pl.ds(ask_ref[k * 8 + t], 1), :]
        return carry

    lax.fori_loop(0, found_ref.shape[0] // 8, gather, 0)


def update(locs, rows, table, accum, asks):
    rows_dev, width = table.shape
    vmem = pl.BlockSpec(memory_space=pltpu.VMEM)
    new_table, new_accum, found = pl.pallas_call(
        update_kernel,
        in_specs=[vmem, vmem, vmem, vmem, pl.BlockSpec(memory_space=pltpu.SMEM)],
        out_specs=[vmem, vmem, vmem],
        out_shape=[
            jax.ShapeDtypeStruct(table.shape, F32),
            jax.ShapeDtypeStruct((rows_dev // 128, 128), F32),
            jax.ShapeDtypeStruct((asks.shape[0], width), F32),
        ],
        scratch_shapes=[
            pltpu.VMEM((1024, rows.shape[0]), BF),
            pltpu.VMEM((rows.shape[0], 2 * width), BF),
            pltpu.VMEM((1024, width), F32),
        ],
        compiler_params=pltpu.CompilerParams(vmem_limit_bytes=48 << 20),
        name="update",
    )(locs.reshape(1, -1), rows, table, accum.reshape(rows_dev // 128, 128), asks)
    return new_table, new_accum.reshape(rows_dev), found


def pick_kernel(index_ref, rows_ref, out_ref):
    def gather(k, carry):
        for t in range(8):
            out_ref[pl.ds(k * 8 + t, 1), :] = rows_ref[pl.ds(index_ref[k * 8 + t], 1), :]
        return carry

    lax.fori_loop(0, out_ref.shape[0] // 8, gather, 0)


def pick(rows, index):
    vmem = pl.BlockSpec(memory_space=pltpu.VMEM)
    return pl.pallas_call(
        pick_kernel,
        in_specs=[pl.BlockSpec(memory_space=pltpu.SMEM), vmem],
        out_specs=vmem,
        out_shape=jax.ShapeDtypeStruct((index.shape[0], rows.shape[1]), F32),
        compiler_params=pltpu.CompilerParams(vmem_limit_bytes=32 << 20),
        name="pick",
    )(index, rows)


def exchange(parts):
    return lax.all_to_all(parts, ("group", "member"), split_axis=0, concat_axis=0, tiled=True)


def local(
    embeddings,
    cot_first,
    cot_second,
    cot_third,
    w_first,
    w_second,
    w_third,
    unique_ids,
    inverse,
    table,
    accum,
    next_ids,
):
    rows_dev, width = table.shape
    owners = lax.axis_size("group") * lax.axis_size("member")
    owner, within, inside = ranks(unique_ids[0], CAP, rows_dev)
    target = owner * CAP + within
    ask_owner, ask_within, ask_inside = ranks(next_ids[0], RCAP, rows_dev)
    ask_target = ask_owner * RCAP + ask_within
    numbers = jnp.concatenate(
        [
            by_owner(owner, within, inside, owners, CAP),
            by_owner(ask_owner, ask_within, ask_inside, owners, RCAP),
        ],
        axis=1,
    )
    numbers = exchange(numbers)
    locs = numbers[:, :CAP].reshape(-1)
    asks = jnp.maximum(numbers[:, CAP:], 0).reshape(-1)

    grads = cin(embeddings, cot_first, cot_second, cot_third, w_first, w_second, w_third)
    send = merge(grads, inverse, target, owners * CAP)
    rows = exchange(send.reshape(owners, CAP, width)).reshape(-1, width)
    new_table, new_accum, found = update(locs, rows, table, accum, asks)
    answers = exchange(found.reshape(owners, RCAP, width)).reshape(-1, width)
    return (new_table, new_accum, pick(answers, ask_target)[None])


def solution(mesh):
    in_specs = (
        P(("group", "member"), None, None),
        P(("group", "member"), None),
        P(("group", "member"), None),
        P(("group", "member"), None),
        P(),
        P(),
        P(),
        P(("group", "member"), None),
        P(("group", "member"), None),
        P(("group", "member"), None),
        P(("group", "member")),
        P(("group", "member"), None),
    )
    out_specs = (
        P(("group", "member"), None),
        P(("group", "member")),
        P(("group", "member"), None, None),
    )
    return jax.shard_map(local, mesh=mesh, in_specs=in_specs, out_specs=out_specs, check_vma=False)
```

time: 342 us -> 168 us (0.49)
  local copies, waits for them, and re-layouts: 155 us -> 24.3 us
  matrix products: 53.6 us -> 0.87 us
  Pallas kernels: 0 us -> 47.3 us
  blocking collectives: 0 us -> 37.7 us
  waiting for transfers between devices: 53.3 us -> 18.3 us
  other arithmetic: 27.6 us -> 6.18 us
  starting transfers between devices: 48.5 us -> 31.4 us
    gather x23 -> x0, local copies, waits for them, and re-layouts: 133 us -> none  [the longest x21 124 us: bucket(): leading = jnp.searchsorted(owner_of, owner_of, side='left')]
    dot_general x56 -> x3, matrix products: 53.6 us -> 0.87 us  [the longest x2 0.59 us: by_owner(): found = jnp.dot(hot, value, preferred_element_type=F32)]
    pallas_call x0 -> x4, Pallas kernels: none -> 47.3 us  [the longest x1 33.2 us: cin(): pl.pallas_call(kernel, grid=(samples // 2,), in_specs=[per(2, FP, width),...]
    all_to_all x0 -> x1, blocking collectives: none -> 37.7 us  [exchange(): lax.all_to_all(parts, ('group', 'member'), split_axis=0, concat_axis=0, t...]
    all_to_all x4 -> x2, waiting for transfers between devices: 53.3 us -> 18.3 us  [exchange(): lax.all_to_all(parts, ('group', 'member'), split_axis=0, concat_axis=0, t...]
    all_to_all x4 -> x2, starting transfers between devices: 48.5 us -> 31.4 us  [exchange(): lax.all_to_all(parts, ('group', 'member'), split_axis=0, concat_axis=0, t...]
    scatter-add x2 -> x0, other arithmetic: 15.5 us -> none  [the longest x1 9 us: local(): jax.ops.segment_sum(grads, inverse.reshape(-1), num_segments=listed.shape...]
    scatter x3 -> x0, local copies, waits for them, and re-layouts: 14.5 us -> none  [the longest x1 6.18 us: local(): ask_local = jnp.full((owners * RCAP,), rows_dev, jnp.int32).at[ask_target...]
  transfers between devices with their start and end apart: 4 -> 2, of which waited for: 2 -> 1; matrix products, arithmetic and copies ran while one was open for 52% -> 13% of each run, Pallas kernels for 0% -> 21%
where the time goes in v1:
time: 168 us; the launch traced here: 167 us
  Pallas kernels  47.3 us (28%)
  blocking collectives  37.7 us (22%)
  starting transfers between devices  31.4 us (19%)
  local copies, waits for them, and re-layouts  24.3 us (14%)
  waiting for transfers between devices  18.3 us (11%)
  other arithmetic  6.18 us (4%)
    all_to_all x1, blocking collectives, exchange(): lax.all_to_all(parts, ('group', 'member'), split_axis=0, concat_axis=0, t...  37.7 us
    pallas_call x1, Pallas kernels, cin(): pl.pallas_call(kernel, grid=(samples // 2,), in_specs=[per(2, FP, width),...  33.2 us
    all_to_all x2, starting transfers between devices, exchange(): lax.all_to_all(parts, ('group', 'member'), split_axis=0, concat_axis=0, t...  31.4 us
    all_to_all x2, waiting for transfers between devices, exchange(): lax.all_to_all(parts, ('group', 'member'), split_axis=0, concat_axis=0, t...  18.3 us
    unnamed x33, local copies, waits for them, and re-layouts  8.65 us
    pallas_call x1, Pallas kernels, update(): pl.pallas_call(update_kernel, in_specs=[vmem, vmem, vmem, vmem, pl.BlockS...  8.16 us
    pallas_call x1, Pallas kernels, pick(): pl.pallas_call(pick_kernel, in_specs=[pl.BlockSpec(memory_space=pltpu.SME...  3.63 us
  transfers between devices with their start and end apart: 2, of which 1 were waited for; matrix products, arithmetic and copies ran while one was open for 13% of the time, Pallas kernels for 21%

profile of v1, /device:TPU:1, one launch (start us, length us, event | category | flops | bytes accessed | tf_op | source)
XLA Modules:
  0.0 167.0 jit_solution(4231076434362680811)
XLA Ops:
  0.7 0.9 fusion.39
  2.1 0.7 fusion.40
  3.2 0.8 copy.41
  4.0 16.6 %all-to-all-start = ((s32[256,1,12]{2,1,0:T(1,128)}), s32[256,1,12]{2,1,0:T(1,128)}, u32[]{:S(2)}, u32[]{:S(2)}) async-start(s32[256,1,12]{2,1,0:T(1,128)} %copy.41), calls=%async_computation | async-start | bytes 262144 | tf_op jit(solution)/shard_map/all_to_all | solution.py:297
  22.1 1.0 fusion.38
  23.1 0.8 fusion.4
  23.9 0.8 fusion.41.refs_6_
  24.7 0.6 pad_convert_fusion.3
  26.0 1.4 copy.52.refs_3_
  27.4 1.1 copy.51
  28.5 2.4 %copy.53.refs_4_ = bf16[32,112,48]{2,1,0:T(8,128)(2,1)} copy(bf16[32,112,48]{1,2,0:T(8,128)(2,1)} %fusion.4) | data formatting | bytes 688128 | tf_op jit(solution)/shard_map/convert_element_type | solution.py:19
  30.9 1.8 %copy.56 = bf16[39,100,100]{2,1,0:T(8,128)(2,1)} copy(bf16[39,100,100]{1,0,2:T(8,128)(2,1)S(1)} %bitcast.64) | data formatting | bytes 1560000
  32.7 1.4 pad.47.clone
  34.1 1.8 %copy.54.refs_8_ = bf16[112,4368]{1,0:T(8,128)(2,1)} copy(bf16[112,4368]{0,1:T(8,128)(2,1)S(1)} %bitcast.60) | data formatting | bytes 1956864 | tf_op jit(solution)/shard_map/slice | solution.py:132
  36.3 1.0 copy.43
  37.4 2.0 %copy.44 = f32[16,2,112]{1,2,0:T(8,128)} copy(f32[16,2,112]{2,1,0:T(2,128)} %bitcast.74) | data formatting | bytes 28672 | tf_op jit(solution)/shard_map/transpose | solution.py:123
  39.4 1.1 copy.42
  40.5 0.8 pad.42.refs_0_
  41.4 1.2 copy-done.1
  42.6 1.1 copy-done.2
  43.7 1.0 copy-done.4
  44.7 1.0 copy-done.5
  45.7 1.0 copy-done.6
  46.7 33.2 %cin.1 = f32[32,40,128]{2,1,0:T(8,128)S(1)} custom-call(bf16[32,48,128]{2,1,0:T(8,128)(2,1)S(1)} %copy-done.4, f32[16,112,2]{2,1,0:T(8,128)S(1)} %bitcast.53, f32[16,112,2]{2,1,0:T(8,128)S(1)} %bitcast.54, bf16[32,112,48]{2,1,0:T(8,128)(2,1)S(1)} %copy.52.refs_3_, bf16[32,112,48]{2,1,0:T(8,128)(2,1)} %copy.53.refs_4_, bf16[32,48,112]{2,1,0:T(8,128)(2,1)S(1)} %copy-done.5, ...), custom_call_target="tpu_custom_call" | custom-call | tf_op jit(solution)/shard_map/cin/pallas_call | solution.py:149
  80.0 2.3 %merge.1 = f32[1024,128]{1,0:T(8,128)} custom-call(s32[1,1280]{1,0:T(1,128)S(1)} %reshape.127.inv_ref, s32[1,768]{1,0:T(1,128)S(1)} %reshape.128.target_ref, f32[1280,128]{1,0:T(8,128)S(1)} %bitcast.56), custom_call_target="tpu_custom_call" | custom-call | tf_op jit(solution)/shard_map/merge/pallas_call | solution.py:213
  82.3 14.7 %all-to-all-start.1 = ((f32[256,4,128]{2,1,0:T(4,128)}), f32[256,4,128]{2,1,0:T(4,128)}, u32[]{:S(2)}, u32[]{:S(2)}) async-start(f32[256,4,128]{2,1,0:T(4,128)} %bitcast.19), calls=%async_computation.1 | async-start | bytes 1048576 | tf_op jit(solution)/shard_map/all_to_all | solution.py:297
  97.0 1.0 slice_maximum_fusion
  98.1 1.0 reshape_reshape.3.loc_ref
  99.1 18.3 %all-to-all-done.1 = f32[256,4,128]{2,1,0:T(4,128)} async-done(((f32[256,4,128]{2,1,0:T(4,128)}), f32[256,4,128]{2,1,0:T(4,128)}, u32[]{:S(2)}, u32[]{:S(2)}) %all-to-all-start.1) | async-done | bytes 524320 | tf_op jit(solution)/shard_map/all_to_all | solution.py:297
  117.5 8.2 %update.1 = (f32[4096,128]{1,0:T(8,128)}, f32[32,128]{1,0:T(8,128)}, f32[2048,128]{1,0:T(8,128)S(1)}) custom-call(s32[1,1024]{1,0:T(1,128)S(1)} %reshape_reshape.3.loc_ref, f32[1024,128]{1,0:T(8,128)} %bitcast.20.rows_ref, f32[4096,128]{1,0:T(8,128)S(1)} %copy-done.3, f32[32,128]{1,0:T(8,128)S(1)} %bitcast.59, s32[2048]{0:T(1024)S(1)} %reshape.138.ask_ref), custom_call_target="tpu_custom_call" | custom-call | tf_op jit(solution)/shard_map/update/pallas_call | solution.py:255
  125.7 37.7 %all_to_all.22 = f32[256,8,128]{2,1,0:T(8,128)S(1)} all-to-all(f32[256,8,128]{2,1,0:T(8,128)S(1)} %bitcast.58), channel_id=1, replica_groups=mesh['group'=4,'member'=64] {'group','member'}, dimensions={0} | all-to-all | bytes 2097152 | tf_op jit(solution)/shard_map/all_to_all | solution.py:297
  163.3 3.6 %pick.1 = f32[1536,128]{1,0:T(8,128)} custom-call(s32[1536]{0:T(1024)S(1)} %get-tuple-element.13.index_ref, f32[2048,128]{1,0:T(8,128)S(1)} %bitcast.52), custom_call_target="tpu_custom_call" | custom-call | tf_op jit(solution)/shard_map/pick/pallas_call | solution.py:286
  (53 shorter events, 3.7 us)
Async XLA Ops:
  0.6 20.5 %copy-start = (bf16[100,100,39]{1,2,0:T(8,128)(2,1)S(1)}, bf16[100,100,39]{1,2,0:T(8,128)(2,1)}, u32[]{:S(2)}) copy-start(bf16[100,100,39]{1,2,0:T(8,128)(2,1)} %param.18) | copy-start | bytes 2340004
  0.6 20.0 %copy-start.9 = (bf16[100,39,39]{0,2,1:T(8,128)(2,1)S(1)}, bf16[100,39,39]{0,2,1:T(8,128)(2,1)}, u32[]{:S(2)}) copy-start(bf16[100,39,39]{0,2,1:T(8,128)(2,1)} %param.16) | copy-start | bytes 912604
  4.0 78.3 %all-to-all-start = ((s32[256,1,12]{2,1,0:T(1,128)}), s32[256,1,12]{2,1,0:T(1,128)}, u32[]{:S(2)}, u32[]{:S(2)}) async-start(s32[256,1,12]{2,1,0:T(1,128)} %copy.41), calls=%async_computation | async-start | bytes 262144 | tf_op jit(solution)/shard_map/all_to_all | solution.py:297
  20.7 0.7 copy-start.12
  22.1 2.6 %copy-start.13 = (bf16[32,100]{1,0:T(8,128)(2,1)S(1)}, bf16[32,100]{1,0:T(8,128)(2,1)}, u32[]{:S(2)}) copy-start(bf16[32,100]{1,0:T(8,128)(2,1)} %param.13) | copy-start | bytes 19204
  23.1 2.4 %copy-start.14 = (bf16[32,100]{1,0:T(8,128)(2,1)S(1)}, bf16[32,100]{1,0:T(8,128)(2,1)}, u32[]{:S(2)}) copy-start(bf16[32,100]{1,0:T(8,128)(2,1)} %param.14) | copy-start | bytes 19204
  28.5 2.4 %copy-start.10 = (bf16[100,100,39]{1,2,0:T(8,128)(2,1)S(1)}, bf16[100,100,39]{1,2,0:T(8,128)(2,1)}, u32[]{:S(2)}) copy-start(bf16[100,100,39]{1,2,0:T(8,128)(2,1)} %param.17) | copy-start | bytes 2340004
  34.1 1.9 %copy-start.8 = (bf16[39,112,128]{2,1,0:T(8,128)(2,1)}, bf16[39,112,128]{2,1,0:T(8,128)(2,1)S(1)}, u32[]{:S(2)}) copy-start(bf16[39,112,128]{2,1,0:T(8,128)(2,1)S(1)} %pad.47.clone) | copy-start | bytes 3354628
  36.3 5.0 %copy-start.11 = (s32[32,39]{1,0:T(8,128)S(1)}, s32[32,39]{1,0:T(8,128)}, u32[]{:S(2)}) copy-start(s32[32,39]{1,0:T(8,128)} %param.20) | copy-start | bytes 14980
  41.4 1.2 copy-start.1
  42.6 1.1 copy-start.2
  43.7 1.0 copy-start.4
  44.7 1.0 copy-start.5
  45.7 1.0 copy-start.6
  79.9 37.5 %copy-start.3 = (f32[4096,128]{1,0:T(8,128)S(1)}, f32[4096,128]{1,0:T(8,128)}, u32[]{:S(2)}) copy-start(f32[4096,128]{1,0:T(8,128)} %table_ref.1) | copy-start | bytes 6291460
  80.0 37.5 %copy-start.7 = (f32[4096]{0:T(1024)S(1)}, f32[4096]{0:T(1024)}, u32[]{:S(2)}) copy-start(f32[4096]{0:T(1024)} %param.22) | copy-start | bytes 49156
  82.3 35.2 %all-to-all-start.1 = ((f32[256,4,128]{2,1,0:T(4,128)}), f32[256,4,128]{2,1,0:T(4,128)}, u32[]{:S(2)}, u32[]{:S(2)}) async-start(f32[256,4,128]{2,1,0:T(4,128)} %bitcast.19), calls=%async_computation.1 | async-start | bytes 1048576 | tf_op jit(solution)/shard_map/all_to_all | solution.py:297

commit v2 on v1

--- a/solution.py
+++ b/solution.py
@@ -33,7 +33,7 @@
 
 def cin_kernel(
     fields,
-    e_ref, c1_ref, c2_ref, thi_ref, tlo_ref, uhi_ref, ulo_ref,
+    e_ref, c1_ref, c2_ref, top_ref,
     w1f_ref, w2f_ref, w2b_ref, w1b_ref,
     out_ref,
     ef, p1, p2, l1f, mid, bot, part, l2s,
@@ -48,7 +48,9 @@
 
     uppers = []
     for s in range(2):
-        grad_two = dot(thi_ref[s], e_ref[s]) + dot(tlo_ref[s], e_ref[s])
+        hi, lo = halves(top_ref[s])
+        rest = (top_ref[s] - hi.astype(F32) - lo.astype(F32)).astype(BF)
+        grad_two = dot(hi, e_ref[s]) + (dot(lo, e_ref[s]) + dot(rest, e_ref[s]))
         uppers.append((c2_ref[0, :, s : s + 1] + grad_two).astype(BF))
     upper = jnp.concatenate(uppers, axis=1)
     upper = jnp.concatenate([upper, jnp.zeros((KP - HP, lanes), BF)], axis=0)
@@ -86,10 +88,11 @@
                 acc[s] = acc[s] + m * b[None]
                 part[j, :, ls] = jnp.sum(m * one, axis=0)
     l2 = l2s[...].astype(BF)
-    bases = [
-        dot(uhi_ref[s], l2[:, s * 128 : (s + 1) * 128]) + dot(ulo_ref[s], l2[:, s * 128 : (s + 1) * 128])
-        for s in range(2)
-    ]
+    bases = []
+    for s in range(2):
+        hi, lo = halves(top_ref[s].T)
+        both = l2[:, s * 128 : (s + 1) * 128]
+        bases.append(dot(hi, both) + dot(lo, both))
     lower = jnp.concatenate(
         [(c1_ref[0, :HQ, s : s + 1] + acc[s].reshape(HQ, 128)).astype(F32) for s in range(2)], axis=1
     )
@@ -122,10 +125,8 @@
         cot = jnp.pad(cot.astype(F32), ((0, 0), (0, HP - maps)))
         return jnp.transpose(cot.reshape(samples // 2, 2, HP), (0, 2, 1))
 
+    w_third = jnp.pad(w_third, ((0, 0), (0, HP - maps), (0, FP - fields)))
     top = jnp.einsum("hij,nh->nij", w_third, cot_third, preferred_element_type=F32)
-    top = jnp.pad(top, ((0, 0), (0, HP - maps), (0, FP - fields)))
-    thi, tlo = halves(top)
-    uhi, ulo = jnp.swapaxes(thi, 1, 2), jnp.swapaxes(tlo, 1, 2)
 
     w2b = jnp.pad(jnp.transpose(w_second, (2, 1, 0)), ((0, 0), (0, HP - maps), (0, KP - maps)))
     w2b = w2b.reshape(fields * HP, KP)
@@ -151,7 +152,7 @@
         grid=(samples // 2,),
         in_specs=[
             per(2, FP, width), per(1, HP, 2), per(1, HP, 2),
-            per(2, HP, FP), per(2, HP, FP), per(2, FP, HP), per(2, FP, HP),
+            per(2, HP, FP),
             whole(w1f), whole(w2f), whole(w2b), whole(w1b),
         ],
         out_specs=per(2, FQ, width),
@@ -168,7 +169,7 @@
         ],
         compiler_params=pltpu.CompilerParams(vmem_limit_bytes=48 << 20),
         name="cin",
-    )(e, columns(cot_first), columns(cot_second), thi, tlo, uhi, ulo, w1f, w2f, w2b, w1b)
+    )(e, columns(cot_first), columns(cot_second), top, w1f, w2f, w2b, w1b)
 
 
 def ranks(row_list, capacity, rows_dev):
@@ -189,46 +190,122 @@
     return (found[:, :capacity] * 64 + found[:, capacity:]).astype(jnp.int32) - 1
 
 
-def merge_kernel(inv_ref, target_ref, grads_ref, out_ref, hot, pair):
-    count, listed = pair.shape[0], target_ref.shape[1]
-    pair[...] = jnp.concatenate(halves(grads_ref[...]), axis=1)
+MESH = pl.DeviceIdType.MESH
+COPIES = 77
+
+
+def moved(step):
+    group, member = lax.axis_index("group"), lax.axis_index("member")
+    x, z, core = member // 16, (member // 2) % 8, member % 2
+    x = (x + (step // 16) % 4) % 4
+    z = (z + (step // 2) % 8) % 8
+    return (group + step // 64) % 4, x * 16 + z * 2 + (core + step % 2) % 2
+
+
+class Tree:
+    def __init__(self):
+        self.sem = pltpu.get_barrier_semaphore()
+        self.group, member = lax.axis_index("group"), lax.axis_index("member")
+        self.x, self.rest = member // 16, member % 16
+        top = self.group * 4 + self.x
+        self.root = jnp.logical_and(top == 0, self.rest == 0)
+        self.leader = jnp.logical_and(top != 0, self.rest == 0)
+
+    def signal(self, group, member):
+        pl.semaphore_signal(self.sem, inc=1, device_id=(group, member), device_id_type=MESH)
+
+    def arrive(self):
+        @pl.when(self.rest != 0)
+        def _():
+            self.signal(self.group, self.x * 16)
+
+    def pass_up(self):
+        @pl.when(self.leader)
+        def _():
+            pl.semaphore_wait(self.sem, 15)
+            self.signal(0, 0)
+
+    def turn(self):
+        @pl.when(self.root)
+        def _():
+            pl.semaphore_wait(self.sem, 30)
+
+            def tell(k, carry):
+                self.signal(k // 4, (k % 4) * 16)
+                return carry
+
+            lax.fori_loop(1, 16, tell, 0)
+
+    def release(self):
+        @pl.when(jnp.logical_not(self.root))
+        def _():
+            pl.semaphore_wait(self.sem, 1)
+
+        @pl.when(self.rest == 0)
+        def _():
+            def tell(k, carry):
+                self.signal(self.group, self.x * 16 + k)
+                return carry
+
+            lax.fori_loop(1, 16, tell, 0)
+
+
+def step_kernel(
+    inv_ref, target_ref, grads_ref, numbers_ref, table_ref, accum_ref,
+    nt_ref, na_ref, answers_ref,
+    hot, pair, grad, send, rows, found, ask_v, ask_s, rows_out, rows_in, answers_out, answers_in, own,
+):
+    tree = Tree()
+    tree.arrive()
+    owners, width = numbers_ref.shape
+    me = lax.axis_index("group") * 64 + lax.axis_index("member")
+    count, listed = inv_ref.shape[1], target_ref.shape[1]
+
+    g = jnp.concatenate(halves(grads_ref[...]), axis=1)
     merged = []
-    rows = 256
-    for b in range(listed // rows):
-        place = lax.broadcasted_iota(jnp.int32, (rows, count), 0) + b * rows
-        hot[...] = jnp.where(place == inv_ref[...], 1.0, 0.0).astype(BF)
-        m = dot(hot[...], pair[...])
-        merged.append(m[:, :128] + m[:, 128:])
+    for b in range(listed // 256):
+        place = lax.broadcasted_iota(jnp.int32, (256, count), 0) + b * 256
+        m = dot(jnp.where(place == inv_ref[...], 1.0, 0.0).astype(BF), g)
+        merged.append(m[:, :width] + m[:, width:])
     merged = jnp.concatenate(halves(jnp.concatenate(merged, axis=0)), axis=1)
-    for b in range(out_ref.shape[0] // rows):
-        place = lax.broadcasted_iota(jnp.int32, (rows, listed), 0) + b * rows
+    tree.pass_up()
+    for c in range(CAP):
+        place = lax.broadcasted_iota(jnp.int32, (owners, listed), 0) + c * owners
         m = dot(jnp.where(place == target_ref[...], 1.0, 0.0).astype(BF), merged)
-        out_ref[b * rows : (b + 1) * rows, :] = m[:, :128] + m[:, 128:]
-
-
-def merge(grads, inverse, target, slots):
-    samples, padded, width = grads.shape
-    inv = jnp.pad(inverse, ((0, 0), (0, padded - inverse.shape[1])), constant_values=-1).reshape(1, -1)
-    count = samples * padded
-    return pl.pallas_call(
-        merge_kernel,
-        out_shape=jax.ShapeDtypeStruct((slots, width), F32),
-        scratch_shapes=[pltpu.VMEM((256, count), BF), pltpu.VMEM((count, 2 * width), BF)],
-        compiler_params=pltpu.CompilerParams(vmem_limit_bytes=32 << 20),
-        name="merge",
-    )(inv, target.reshape(1, -1), grads.reshape(count, width))
-
-
-def update_kernel(loc_ref, rows_ref, table_ref, accum_ref, ask_ref, nt_ref, na_ref, found_ref, hot, pair, grad):
-    pair[...] = jnp.concatenate(halves(rows_ref[...]), axis=1)
-    got = pair.shape[0]
+        send[:, c, :] = m[:, :width] + m[:, width:]
+    send[:, CAP, :] = numbers_ref[...]
+    tree.turn()
+    rows[me] = send[me]
+    tree.release()
+
+    def send_rows(k, carry):
+        group, member = moved((k * COPIES) % owners)
+        pltpu.make_async_remote_copy(
+            src_ref=send.at[group * 64 + member], dst_ref=rows.at[me],
+            send_sem=rows_out, recv_sem=rows_in,
+            device_id=(group, member), device_id_type=MESH,
+        ).start()
+        return carry
+
+    lax.fori_loop(1, owners, send_rows, 0)
+    others = pl.ds(0, owners - 1)
+    pltpu.make_async_copy(send.at[others], rows.at[others], rows_in).wait()
+
+    numbers = rows[:, CAP, :].T[:16].astype(jnp.int32)
+    ask_v[...] = jnp.clip(numbers, 0, table_ref.shape[0] - 1)
+    to_scalars = pltpu.make_async_copy(ask_v, ask_s, own)
+    to_scalars.start()
+    for c in range(CAP):
+        pair[c * owners : (c + 1) * owners, :] = jnp.concatenate(halves(rows[:, c, :]), axis=1)
     lane = lax.broadcasted_iota(jnp.int32, (128, 128), 1)
     for b in range(table_ref.shape[0] // 1024):
         for r in range(8):
-            place = lax.broadcasted_iota(jnp.int32, (128, got), 0) + (b * 1024 + r * 128)
-            hot[r * 128 : (r + 1) * 128, :] = jnp.where(place == loc_ref[...], 1.0, 0.0).astype(BF)
-        g = dot(hot[...], pair[...])
-        grad[...] = g[:, :128] + g[:, 128:]
+            place = lax.broadcasted_iota(jnp.int32, (128, owners), 0) + (b * 1024 + r * 128)
+            for c in range(CAP):
+                hit = place == numbers[c : c + 1, :]
+                hot[r * 128 : (r + 1) * 128, c * owners : (c + 1) * owners] = jnp.where(hit, 1.0, 0.0).astype(BF)
+        s = dot(hot[...], pair[...])
+        grad[...] = s[:, :width] + s[:, width:]
         means = jnp.zeros((128, 128), F32)
         for r in range(8):
             part = grad[r * 128 : (r + 1) * 128, :]
@@ -240,36 +317,86 @@
         for r in range(8):
             at = slice(b * 1024 + r * 128, b * 1024 + (r + 1) * 128)
             nt_ref[at, :] = table_ref[at, :] - grad[r * 128 : (r + 1) * 128, :] * scale[:, r : r + 1]
-
-    def gather(k, carry):
-        for t in range(8):
-            found_ref[pl.ds(k * 8 + t, 1), :] = nt_ref[pl.ds(ask_ref[k * 8 + t], 1), :]
+    to_scalars.wait()
+
+    def look_up(p, out):
+        for t in range(RCAP):
+            row = jnp.clip(ask_s[CAP + t, p], 0, nt_ref.shape[0] - 1)
+            out[p, t : t + 1, :] = nt_ref[pl.ds(row, 1), :]
+
+    late = 4
+
+    def gather(k):
+        group, member = moved((k * COPIES) % owners)
+        look_up(group * 64 + member, found)
+
+    def send_answers(k):
+        group, member = moved((k * COPIES) % owners)
+        pltpu.make_async_remote_copy(
+            src_ref=found.at[group * 64 + member], dst_ref=answers_ref.at[me],
+            send_sem=answers_out, recv_sem=answers_in,
+            device_id=(group, member), device_id_type=MESH,
+        ).start()
+
+    def first(k, carry):
+        gather(k)
         return carry
 
-    lax.fori_loop(0, found_ref.shape[0] // 8, gather, 0)
-
-
-def update(locs, rows, table, accum, asks):
-    rows_dev, width = table.shape
+    def both(k, carry):
+        gather(k)
+        send_answers(k - late)
+        return carry
+
+    def last(k, carry):
+        send_answers(k)
+        return carry
+
+    lax.fori_loop(1, 1 + late, first, 0)
+    lax.fori_loop(1 + late, owners, both, 0)
+    look_up(me, answers_ref)
+    lax.fori_loop(owners - late, owners, last, 0)
+    pltpu.make_async_copy(send.at[others], rows.at[others], rows_out).wait()
+    pltpu.make_async_copy(found.at[others], answers_ref.at[others], answers_in).wait()
+    pltpu.make_async_copy(found.at[others], answers_ref.at[others], answers_out).wait()
+
+
+def step(grads, inverse, target, numbers, table, accum):
+    samples, padded, width = grads.shape
+    owners = numbers.shape[0]
+    rows_dev = table.shape[0]
+    inv = jnp.pad(inverse, ((0, 0), (0, padded - inverse.shape[1])), constant_values=-1).reshape(1, -1)
     vmem = pl.BlockSpec(memory_space=pltpu.VMEM)
-    new_table, new_accum, found = pl.pallas_call(
-        update_kernel,
-        in_specs=[vmem, vmem, vmem, vmem, pl.BlockSpec(memory_space=pltpu.SMEM)],
-        out_specs=[vmem, vmem, vmem],
+    new_table, new_accum, answers = pl.pallas_call(
+        step_kernel,
+        in_specs=[vmem] * 6,
+        out_specs=[vmem] * 3,
         out_shape=[
             jax.ShapeDtypeStruct(table.shape, F32),
             jax.ShapeDtypeStruct((rows_dev // 128, 128), F32),
-            jax.ShapeDtypeStruct((asks.shape[0], width), F32),
+            jax.ShapeDtypeStruct((owners, RCAP, width), F32),
         ],
         scratch_shapes=[
-            pltpu.VMEM((1024, rows.shape[0]), BF),
-            pltpu.VMEM((rows.shape[0], 2 * width), BF),
+            pltpu.VMEM((1024, CAP * owners), BF),
+            pltpu.VMEM((CAP * owners, 2 * width), BF),
             pltpu.VMEM((1024, width), F32),
+            pltpu.VMEM((owners, CAP + 1, width), F32),
+            pltpu.VMEM((owners, CAP + 1, width), F32),
+            pltpu.VMEM((owners, RCAP, width), F32),
+            pltpu.VMEM((16, owners), jnp.int32),
+            pltpu.SMEM((16, owners), jnp.int32),
+            pltpu.SemaphoreType.DMA,
+            pltpu.SemaphoreType.DMA,
+            pltpu.SemaphoreType.DMA,
+            pltpu.SemaphoreType.DMA,
+            pltpu.SemaphoreType.DMA,
         ],
-        compiler_params=pltpu.CompilerParams(vmem_limit_bytes=48 << 20),
-        name="update",
-    )(locs.reshape(1, -1), rows, table, accum.reshape(rows_dev // 128, 128), asks)
-    return new_table, new_accum.reshape(rows_dev), found
+        compiler_params=pltpu.CompilerParams(
+            collective_id=0, has_side_effects=True, vmem_limit_bytes=56 << 20
+        ),
+        name="step",
+    )(inv, target.reshape(1, -1), grads.reshape(samples * padded, width), numbers, table,
+      accum.reshape(rows_dev // 128, 128))
+    return new_table, new_accum.reshape(rows_dev), answers
 
 
 def pick_kernel(index_ref, rows_ref, out_ref):
@@ -291,10 +418,6 @@
         compiler_params=pltpu.CompilerParams(vmem_limit_bytes=32 << 20),
         name="pick",
     )(index, rows)
-
-
-def exchange(parts):
-    return lax.all_to_all(parts, ("group", "member"), split_axis=0, concat_axis=0, tiled=True)
 
 
 def local(
@@ -314,7 +437,7 @@
     rows_dev, width = table.shape
     owners = lax.axis_size("group") * lax.axis_size("member")
     owner, within, inside = ranks(unique_ids[0], CAP, rows_dev)
-    target = owner * CAP + within
+    target = within * owners + owner
     ask_owner, ask_within, ask_inside = ranks(next_ids[0], RCAP, rows_dev)
     ask_target = ask_owner * RCAP + ask_within
     numbers = jnp.concatenate(
@@ -324,16 +447,10 @@
         ],
         axis=1,
     )
-    numbers = exchange(numbers)
-    locs = numbers[:, :CAP].reshape(-1)
-    asks = jnp.maximum(numbers[:, CAP:], 0).reshape(-1)
-
+    numbers = jnp.pad(numbers.astype(F32), ((0, 0), (0, width - CAP - RCAP)))
     grads = cin(embeddings, cot_first, cot_second, cot_third, w_first, w_second, w_third)
-    send = merge(grads, inverse, target, owners * CAP)
-    rows = exchange(send.reshape(owners, CAP, width)).reshape(-1, width)
-    new_table, new_accum, found = update(locs, rows, table, accum, asks)
-    answers = exchange(found.reshape(owners, RCAP, width)).reshape(-1, width)
-    return (new_table, new_accum, pick(answers, ask_target)[None])
+    new_table, new_accum, answers = step(grads, inverse, target, numbers, table, accum)
+    return (new_table, new_accum, pick(answers.reshape(-1, width), ask_target)[None])
 
 
 def solution(mesh):

time: 168 us -> 132 us (0.79)
  Pallas kernels: 47.3 us -> 111 us
  blocking collectives: 37.7 us -> 0 us
  starting transfers between devices: 31.4 us -> 0 us
  waiting for transfers between devices: 18.3 us -> 0 us
  local copies, waits for them, and re-layouts: 24.3 us -> 17 us
  other arithmetic: 6.18 us -> 2.28 us
    pallas_call x2 -> x1, Pallas kernels: 10.4 us -> 73.5 us  [step(): pl.pallas_call(step_kernel, in_specs=[vmem] * 6, out_specs=[vmem] * 3, ou...]
    all_to_all x1 -> x0, blocking collectives: 37.7 us -> none  [exchange(): lax.all_to_all(parts, ('group', 'member'), split_axis=0, concat_axis=0, t...]
    all_to_all x2 -> x0, starting transfers between devices: 31.4 us -> none  [exchange(): lax.all_to_all(parts, ('group', 'member'), split_axis=0, concat_axis=0, t...]
    all_to_all x2 -> x0, waiting for transfers between devices: 18.3 us -> none  [exchange(): lax.all_to_all(parts, ('group', 'member'), split_axis=0, concat_axis=0, t...]
    transpose x2, local copies, waits for them, and re-layouts: 3.05 us -> 0.67 us  [columns(): return jnp.transpose(cot.reshape(samples // 2, 2, HP), (0, 2, 1))]
    convert_element_type x1, local copies, waits for them, and re-layouts: 2.37 us -> 0.12 us  [local(): numbers = jnp.pad(numbers.astype(F32), ((0, 0), (0, width - CAP - RCAP)))]
    unnamed x33 -> x32, local copies, waits for them, and re-layouts: 8.65 us -> 9.61 us
  transfers between devices with their start and end apart: 2 -> 0, of which waited for: 1 -> 0; matrix products, arithmetic and copies ran while one was open for 13% -> 0% of each run, Pallas kernels for 21% -> 0%
where the time goes in v2:
time: 132 us
  Pallas kernels  111 us (84%)
  local copies, waits for them, and re-layouts  17 us (13%)
  other arithmetic  2.28 us (2%)
    pallas_call x1, Pallas kernels, step(): pl.pallas_call(step_kernel, in_specs=[vmem] * 6, out_specs=[vmem] * 3, ou...  73.5 us
    pallas_call x1, Pallas kernels, cin(): pl.pallas_call(kernel, grid=(samples // 2,), in_specs=[per(2, FP, width),...  33.5 us
    unnamed x32, local copies, waits for them, and re-layouts  9.61 us
    pallas_call x1, Pallas kernels, pick(): pl.pallas_call(pick_kernel, in_specs=[pl.BlockSpec(memory_space=pltpu.SME...  3.63 us

profile of v2, /device:TPU:1, one launch (start us, length us, event | category | flops | bytes accessed | tf_op | source)
XLA Modules:
  0.0 131.7 jit_solution(2037547691957917419)
XLA Ops:
  0.7 0.8 fusion.38
  1.5 0.1 multiply_add_fusion
  1.7 0.4 fusion
  2.0 0.7 fusion.34
  2.9 0.2 fusion.5
  3.2 0.1 copy.65
  3.3 0.7 pad.53.numbers_ref
  3.9 0.6 reshape.114.target_ref
  4.6 0.2 fusion.3
  5.0 0.1 pad_maximum_fusion
  5.1 1.1 copy.63
  6.2 1.6 %copy.67 = bf16[39,100,100]{2,1,0:T(8,128)(2,1)S(1)} copy(bf16[39,100,100]{1,0,2:T(8,128)(2,1)S(1)} %bitcast.53) | data formatting | bytes 1560000
  7.8 0.2 pad.51.clone
  8.1 1.0 copy.64.refs_5_
  9.1 0.6 copy-done.8
  9.7 0.1 copy.57
  9.9 0.3 fusion.1
  10.2 1.8 %copy.58 = f32[112,48,32]{1,0,2:T(8,128)} copy(f32[112,48,32]{0,2,1:T(8,128)S(1)} %fusion.1) | data formatting | bytes 1376256 | tf_op jit(solution)/shard_map/hij,nh->nij/dot_general | solution.py:129
  12.0 0.1 pad.50.clone
  12.2 0.3 copy.60
  12.4 0.3 copy-done.11
  12.7 0.3 copy.55
  13.0 0.3 copy.56
  13.4 1.2 copy.54
  14.6 33.5 %cin.1 = f32[32,40,128]{2,1,0:T(8,128)S(1)} custom-call(bf16[32,48,128]{2,1,0:T(8,128)(2,1)S(1)} %pad.46.refs_0_, f32[16,112,2]{2,1,0:T(8,128)S(1)} %bitcast.42, f32[16,112,2]{2,1,0:T(8,128)S(1)} %bitcast.43, f32[32,112,48]{2,1,0:T(8,128)} %bitcast.50, bf16[112,1872]{1,0:T(8,128)(2,1)S(1)} %bitcast.46, bf16[112,4368]{1,0:T(8,128)(2,1)S(1)} %copy.64.refs_5_, ...), custom_call_target="tpu_custom_call" | custom-call | tf_op jit(solution)/shard_map/cin/pallas_call | solution.py:150
  48.1 0.8 copy-done.2
  49.0 0.7 reshape.113.inv_ref
  49.7 73.5 %step.1 = (f32[4096,128]{1,0:T(8,128)}, f32[32,128]{1,0:T(8,128)}, f32[256,8,128]{2,1,0:T(8,128)}) custom-call(s32[1,1280]{1,0:T(1,128)} %reshape.113.inv_ref, s32[1,768]{1,0:T(1,128)} %reshape.114.target_ref, f32[1280,128]{1,0:T(8,128)} %bitcast.45, f32[256,128]{1,0:T(8,128)} %pad.53.numbers_ref, f32[4096,128]{1,0:T(8,128)} %table_ref.1, f32[32,128]{1,0:T(8,128)} %bitcast.67), custom_call_target="tpu_custom_call" | custom-call | tf_op jit(solution)/shard_map/step/pallas_call | solution.py:369
  123.2 1.2 copy-done.3
  124.4 3.6 %pick.1 = f32[1536,128]{1,0:T(8,128)} custom-call(s32[1536]{0:T(1024)S(1)} %get-tuple-element.13.index_ref, f32[2048,128]{1,0:T(8,128)S(1)} %bitcast.47), custom_call_target="tpu_custom_call" | custom-call | tf_op jit(solution)/shard_map/pick/pallas_call | solution.py:413
  128.0 3.1 %copy.71 = f32[4096,128]{1,0:T(8,128)} copy(f32[4096,128]{1,0:T(8,128)} %get-tuple-element.32) | data formatting | bytes 4194304
  131.1 0.6 copy.72
  (39 shorter events, 0.7 us)
Async XLA Ops:
  0.6 9.2 %copy-start = (bf16[32,100]{1,0:T(8,128)(2,1)S(1)}, bf16[32,100]{1,0:T(8,128)(2,1)}, u32[]{:S(2)}) copy-start(bf16[32,100]{1,0:T(8,128)(2,1)} %param.15) | copy-start | bytes 19204
  0.6 3.9 %copy-start.5 = (bf16[100,39,39]{0,2,1:T(8,128)(2,1)S(1)}, bf16[100,39,39]{0,2,1:T(8,128)(2,1)}, u32[]{:S(2)}) copy-start(bf16[100,39,39]{0,2,1:T(8,128)(2,1)} %param.16) | copy-start | bytes 912604
  5.0 1.3 copy-start.7
  8.1 1.8 %copy-start.4 = (bf16[39,112,128]{2,1,0:T(8,128)(2,1)}, bf16[39,112,128]{2,1,0:T(8,128)(2,1)S(1)}, u32[]{:S(2)}) copy-start(bf16[39,112,128]{2,1,0:T(8,128)(2,1)S(1)} %pad.51.clone) | copy-start | bytes 3354628
  8.1 1.6 %copy-start.8 = (bf16[100,100,39]{1,2,0:T(8,128)(2,1)S(1)}, bf16[100,100,39]{1,2,0:T(8,128)(2,1)}, u32[]{:S(2)}) copy-start(bf16[100,100,39]{1,2,0:T(8,128)(2,1)} %param.18) | copy-start | bytes 2340004
  10.1 1.8 %copy-start.6 = (bf16[100,39,39]{0,2,1:T(8,128)(2,1)S(1)}, bf16[100,39,39]{0,2,1:T(8,128)(2,1)}, u32[]{:S(2)}) copy-start(bf16[100,39,39]{0,2,1:T(8,128)(2,1)} %param.16) | copy-start | bytes 912604
  12.0 0.7 copy-start.11
  12.0 1.0 copy-start.12
  13.4 1.2 copy-start.1
  14.6 34.3 %copy-start.9 = (s32[32,39]{1,0:T(8,128)S(1)}, s32[32,39]{1,0:T(8,128)}, u32[]{:S(2)}) copy-start(s32[32,39]{1,0:T(8,128)} %param.20) | copy-start | bytes 14980
  48.1 0.8 copy-start.2
  123.2 1.2 copy-start.3
  128.0 3.1 %copy-start.10 = (f32[32,128]{1,0:T(8,128)S(1)}, f32[32,128]{1,0:T(8,128)}, u32[]{:S(2)}) copy-start(f32[32,128]{1,0:T(8,128)} %get-tuple-element.7) | copy-start | bytes 49156

commit v3 on v2

--- a/solution.py
+++ b/solution.py
@@ -5,6 +5,7 @@
 from jax.experimental.pallas import tpu as pltpu
 from jax.sharding import PartitionSpec as P
 
+FIELDS = 39
 CAP = 4
 RCAP = 8
 RATE = 0.5
@@ -31,15 +32,15 @@
 JC = 3
 
 
-def cin_kernel(
-    fields,
-    e_ref, c1_ref, c2_ref, top_ref,
-    w1f_ref, w2f_ref, w2b_ref, w1b_ref,
+def cin_pair(
+    fields, g,
+    e_ref, c1_ref, c2_ref, top_ref, w1f_ref, w2f_ref, w2b_ref, w1b_ref,
     out_ref,
     ef, p1, p2, l1f, mid, bot, part, l2s,
 ):
     lanes = 256
-    e = jnp.concatenate([e_ref[0], e_ref[1]], axis=1)
+    c1, c2 = c1_ref[g], c2_ref[g]
+    e = jnp.concatenate([e_ref[2 * g], e_ref[2 * g + 1]], axis=1)
     ef[...] = e.astype(F32)
     e3 = e.reshape(FP // 16, 16, lanes)
 
@@ -48,10 +49,11 @@
 
     uppers = []
     for s in range(2):
-        hi, lo = halves(top_ref[s])
-        rest = (top_ref[s] - hi.astype(F32) - lo.astype(F32)).astype(BF)
-        grad_two = dot(hi, e_ref[s]) + (dot(lo, e_ref[s]) + dot(rest, e_ref[s]))
-        uppers.append((c2_ref[0, :, s : s + 1] + grad_two).astype(BF))
+        top, one = top_ref[2 * g + s], e[:, s * 128 : (s + 1) * 128]
+        hi, lo = halves(top)
+        rest = (top - hi.astype(F32) - lo.astype(F32)).astype(BF)
+        grad_two = dot(hi, one) + (dot(lo, one) + dot(rest, one))
+        uppers.append((c2[:, s : s + 1] + grad_two).astype(BF))
     upper = jnp.concatenate(uppers, axis=1)
     upper = jnp.concatenate([upper, jnp.zeros((KP - HP, lanes), BF)], axis=0)
 
@@ -90,11 +92,11 @@
     l2 = l2s[...].astype(BF)
     bases = []
     for s in range(2):
-        hi, lo = halves(top_ref[s].T)
+        hi, lo = halves(top_ref[2 * g + s].T)
         both = l2[:, s * 128 : (s + 1) * 128]
         bases.append(dot(hi, both) + dot(lo, both))
     lower = jnp.concatenate(
-        [(c1_ref[0, :HQ, s : s + 1] + acc[s].reshape(HQ, 128)).astype(F32) for s in range(2)], axis=1
+        [(c1[:HQ, s : s + 1] + acc[s].reshape(HQ, 128)).astype(F32) for s in range(2)], axis=1
     )
     lower = jnp.concatenate([lower, jnp.zeros((KP - HQ, lanes), F32)], axis=0).astype(BF)
     lower = jnp.concatenate([lower, lower], axis=0)
@@ -113,10 +115,10 @@
                 part[j, :, ls] = t
     for s in range(2):
         ls = slice(s * 128, (s + 1) * 128)
-        out_ref[s] = jnp.sum(part[:, :, ls], axis=1) + bases[s][:FQ]
-
-
-def cin(embeddings, cot_first, cot_second, cot_third, w_first, w_second, w_third):
+        out_ref[2 * g + s] = jnp.sum(part[:, :, ls], axis=1) + bases[s][:FQ]
+
+
+def cin_operands(embeddings, cot_first, cot_second, cot_third, w_first, w_second, w_third):
     samples, fields, width = embeddings.shape
     maps = cot_first.shape[1]
     e = jnp.pad(embeddings, ((0, 0), (0, FP - fields), (0, 0)))
@@ -137,57 +139,41 @@
     both = both + jnp.swapaxes(both, 1, 2)
     both = jnp.pad(jnp.transpose(both, (2, 1, 0)), ((0, FQ - fields), (0, FQ - fields), (0, KP - maps)))
     w1b = jnp.concatenate(halves(both), axis=2).reshape(FQ * FQ, 2 * KP)
-
-    def per(*shape):
-        return pl.BlockSpec(shape, lambda g: (g,) + (0,) * (len(shape) - 1))
-
-    def whole(x):
-        return pl.BlockSpec(x.shape, lambda g: (0,) * x.ndim, pipeline_mode=pl.Buffered(1))
-
-    def kernel(*refs):
-        cin_kernel(fields, *refs)
-
-    return pl.pallas_call(
-        kernel,
-        grid=(samples // 2,),
-        in_specs=[
-            per(2, FP, width), per(1, HP, 2), per(1, HP, 2),
-            per(2, HP, FP),
-            whole(w1f), whole(w2f), whole(w2b), whole(w1b),
-        ],
-        out_specs=per(2, FQ, width),
-        out_shape=jax.ShapeDtypeStruct((samples, FQ, width), F32),
-        scratch_shapes=[
-            pltpu.VMEM((FP, 256), F32),
-            pltpu.VMEM((fields * FP, 256), BF),
-            pltpu.VMEM((fields * HP, 256), BF),
-            pltpu.VMEM((HP, 256), F32),
-            pltpu.VMEM((2, JC * HP, 256), F32),
-            pltpu.VMEM((2, 8 * FQ, 256), F32),
-            pltpu.VMEM((FQ, 8, 256), F32),
-            pltpu.VMEM((HP, 256), F32),
-        ],
-        compiler_params=pltpu.CompilerParams(vmem_limit_bytes=48 << 20),
-        name="cin",
-    )(e, columns(cot_first), columns(cot_second), top, w1f, w2f, w2b, w1b)
+    return e, columns(cot_first), columns(cot_second), top, w1f, w2f, w2b, w1b
+
+
+def cin_scratch(fields):
+    return [
+        pltpu.VMEM((FP, 256), F32),
+        pltpu.VMEM((fields * FP, 256), BF),
+        pltpu.VMEM((fields * HP, 256), BF),
+        pltpu.VMEM((HP, 256), F32),
+        pltpu.VMEM((2, JC * HP, 256), F32),
+        pltpu.VMEM((2, 8 * FQ, 256), F32),
+        pltpu.VMEM((FQ, 8, 256), F32),
+        pltpu.VMEM((HP, 256), F32),
+    ]
 
 
 def ranks(row_list, capacity, rows_dev):
     owner = row_list // rows_dev
+    lane = lax.broadcasted_iota(jnp.int32, owner.shape, 1)
     within = jnp.zeros_like(owner)
     for k in range(1, capacity):
-        earlier = jnp.concatenate([jnp.full((k,), -1, jnp.int32), owner[:-k]])
-        within = within + (earlier == owner).astype(jnp.int32)
+        same = jnp.logical_and(pltpu.roll(owner, k, 1) == owner, lane >= k)
+        within = within + jnp.where(same, 1, 0)
     return owner, within, row_list - owner * rows_dev
 
 
 def by_owner(owner, within, inside, owners, capacity):
-    hot = (jnp.arange(owners, dtype=jnp.int32)[:, None] == owner[None, :]).astype(BF)
-    places = jnp.arange(capacity, dtype=jnp.int32)[None, :]
-    value = jnp.where(within[:, None] == places, inside[:, None] + 1, 0)
-    value = jnp.concatenate([value // 64, value % 64], axis=1).astype(BF)
-    found = jnp.dot(hot, value, preferred_element_type=F32)
-    return (found[:, :capacity] * 64 + found[:, capacity:]).astype(jnp.int32) - 1
+    hot = lax.broadcasted_iota(jnp.int32, (owners, owner.shape[1]), 0) == owner
+    hot = jnp.where(hot, 1.0, 0.0).astype(BF)
+    place = lax.broadcasted_iota(jnp.int32, (8, owner.shape[1]), 0)
+    value = jnp.where(place == within, inside + 1, 0)
+    high = value // 64
+    value = jnp.concatenate([high.astype(F32), (value - high * 64).astype(F32)], axis=0).astype(BF)
+    found = lax.dot_general(hot, value, (((1,), (1,)), ((), ())), preferred_element_type=F32)
+    return found[:, :8] * 64 + found[:, 8:] - 1
 
 
 MESH = pl.DeviceIdType.MESH
@@ -251,32 +237,55 @@
 
 
 def step_kernel(
-    inv_ref, target_ref, grads_ref, numbers_ref, table_ref, accum_ref,
-    nt_ref, na_ref, answers_ref,
-    hot, pair, grad, send, rows, found, ask_v, ask_s, rows_out, rows_in, answers_out, answers_in, own,
+    inv_ref, ids_ref, next_ref, table_ref, accum_ref,
+    e_ref, c1_ref, c2_ref, top_ref, w1f_ref, w2f_ref, w2b_ref, w1b_ref,
+    nt_out, na_ref, answers_ref,
+    nt_ref, hot, pair, grad, grads, send, rows, found, ask_v, ask_s, rows_out, rows_in, answers_out, answers_in, own, table_in, table_out,
+    *scratch,
 ):
     tree = Tree()
     tree.arrive()
-    owners, width = numbers_ref.shape
+    table_copy = pltpu.make_async_copy(table_ref, nt_ref, table_in)
+    table_copy.start()
+    owners, width = send.shape[0], send.shape[2]
+    rows_dev = table_ref.shape[0]
     me = lax.axis_index("group") * 64 + lax.axis_index("member")
-    count, listed = inv_ref.shape[1], target_ref.shape[1]
-
-    g = jnp.concatenate(halves(grads_ref[...]), axis=1)
+    count, listed = inv_ref.shape[1], ids_ref.shape[1]
+
+    owner, within, inside = ranks(ids_ref[...], CAP, rows_dev)
+    target = within * owners + owner
+    ask_owner, ask_within, ask_inside = ranks(next_ref[...], RCAP, rows_dev)
+    numbers = [
+        by_owner(owner, within, inside, owners, CAP),
+        by_owner(ask_owner, ask_within, ask_inside, owners, RCAP),
+    ]
+    send[:, CAP, :] = jnp.concatenate(numbers + [jnp.zeros((owners, width - 16), F32)], axis=1)
+
+    steps = e_ref.shape[0] // 2
+
+    def cin_step(g, carry):
+        pl.when(g == steps // 4)(tree.pass_up)
+        pl.when(g == steps // 2)(tree.turn)
+        pl.when(g == steps * 3 // 4)(tree.release)
+        cin_pair(
+            FIELDS, g, e_ref, c1_ref, c2_ref, top_ref, w1f_ref, w2f_ref, w2b_ref, w1b_ref, grads, *scratch
+        )
+        return carry
+
+    lax.fori_loop(0, steps, cin_step, 0)
+
+    g = jnp.concatenate(halves(grads[...].reshape(count, width)), axis=1)
     merged = []
     for b in range(listed // 256):
         place = lax.broadcasted_iota(jnp.int32, (256, count), 0) + b * 256
         m = dot(jnp.where(place == inv_ref[...], 1.0, 0.0).astype(BF), g)
         merged.append(m[:, :width] + m[:, width:])
     merged = jnp.concatenate(halves(jnp.concatenate(merged, axis=0)), axis=1)
-    tree.pass_up()
     for c in range(CAP):
         place = lax.broadcasted_iota(jnp.int32, (owners, listed), 0) + c * owners
-        m = dot(jnp.where(place == target_ref[...], 1.0, 0.0).astype(BF), merged)
+        m = dot(jnp.where(place == target, 1.0, 0.0).astype(BF), merged)
         send[:, c, :] = m[:, :width] + m[:, width:]
-    send[:, CAP, :] = numbers_ref[...]
-    tree.turn()
     rows[me] = send[me]
-    tree.release()
 
     def send_rows(k, carry):
         group, member = moved((k * COPIES) % owners)
@@ -292,12 +301,13 @@
     pltpu.make_async_copy(send.at[others], rows.at[others], rows_in).wait()
 
     numbers = rows[:, CAP, :].T[:16].astype(jnp.int32)
-    ask_v[...] = jnp.clip(numbers, 0, table_ref.shape[0] - 1)
+    ask_v[...] = jnp.clip(numbers, 0, rows_dev - 1)
     to_scalars = pltpu.make_async_copy(ask_v, ask_s, own)
     to_scalars.start()
     for c in range(CAP):
         pair[c * owners : (c + 1) * owners, :] = jnp.concatenate(halves(rows[:, c, :]), axis=1)
     lane = lax.broadcasted_iota(jnp.int32, (128, 128), 1)
+    table_copy.wait()
     for b in range(table_ref.shape[0] // 1024):
         for r in range(8):
             place = lax.broadcasted_iota(jnp.int32, (128, owners), 0) + (b * 1024 + r * 128)
@@ -316,12 +326,12 @@
         scale = jnp.concatenate([scale, jnp.zeros((120, 128), F32)], axis=0).T
         for r in range(8):
             at = slice(b * 1024 + r * 128, b * 1024 + (r + 1) * 128)
-            nt_ref[at, :] = table_ref[at, :] - grad[r * 128 : (r + 1) * 128, :] * scale[:, r : r + 1]
+            nt_ref[at, :] = nt_ref[at, :] - grad[r * 128 : (r + 1) * 128, :] * scale[:, r : r + 1]
     to_scalars.wait()
 
     def look_up(p, out):
         for t in range(RCAP):
-            row = jnp.clip(ask_s[CAP + t, p], 0, nt_ref.shape[0] - 1)
+            row = jnp.clip(ask_s[8 + t, p], 0, rows_dev - 1)
             out[p, t : t + 1, :] = nt_ref[pl.ds(row, 1), :]
 
     late = 4
@@ -352,72 +362,108 @@
         return carry
 
     lax.fori_loop(1, 1 + late, first, 0)
+    look_up(me, found)
+    table_back = pltpu.make_async_copy(nt_ref, nt_out, table_out)
+    table_back.start()
     lax.fori_loop(1 + late, owners, both, 0)
-    look_up(me, answers_ref)
+    mine = pltpu.make_async_copy(found.at[me], answers_ref.at[me], own)
+    mine.start()
     lax.fori_loop(owners - late, owners, last, 0)
+    mine.wait()
+    table_back.wait()
     pltpu.make_async_copy(send.at[others], rows.at[others], rows_out).wait()
     pltpu.make_async_copy(found.at[others], answers_ref.at[others], answers_in).wait()
     pltpu.make_async_copy(found.at[others], answers_ref.at[others], answers_out).wait()
 
 
-def step(grads, inverse, target, numbers, table, accum):
-    samples, padded, width = grads.shape
-    owners = numbers.shape[0]
-    rows_dev = table.shape[0]
-    inv = jnp.pad(inverse, ((0, 0), (0, padded - inverse.shape[1])), constant_values=-1).reshape(1, -1)
+def step(inverse, unique_ids, next_ids, table, accum, operands):
+    rows_dev, width = table.shape
+    samples, fields = inverse.shape
+    owners = lax.axis_size("group") * lax.axis_size("member")
+    count = samples * FQ
+    inv = jnp.pad(inverse, ((0, 0), (0, FQ - fields)), constant_values=-1).reshape(1, -1)
     vmem = pl.BlockSpec(memory_space=pltpu.VMEM)
-    new_table, new_accum, answers = pl.pallas_call(
+    return pl.pallas_call(
         step_kernel,
-        in_specs=[vmem] * 6,
-        out_specs=[vmem] * 3,
+        in_specs=[vmem] * 3 + [pl.BlockSpec(memory_space=pl.ANY)] + [vmem] * (1 + len(operands)),
+        out_specs=[pl.BlockSpec(memory_space=pl.ANY), vmem, pl.BlockSpec(memory_space=pl.ANY)],
         out_shape=[
             jax.ShapeDtypeStruct(table.shape, F32),
             jax.ShapeDtypeStruct((rows_dev // 128, 128), F32),
             jax.ShapeDtypeStruct((owners, RCAP, width), F32),
         ],
         scratch_shapes=[
+            pltpu.VMEM(table.shape, F32),
             pltpu.VMEM((1024, CAP * owners), BF),
             pltpu.VMEM((CAP * owners, 2 * width), BF),
             pltpu.VMEM((1024, width), F32),
+            pltpu.VMEM((samples, FQ, width), F32),
             pltpu.VMEM((owners, CAP + 1, width), F32),
             pltpu.VMEM((owners, CAP + 1, width), F32),
             pltpu.VMEM((owners, RCAP, width), F32),
             pltpu.VMEM((16, owners), jnp.int32),
             pltpu.SMEM((16, owners), jnp.int32),
-            pltpu.SemaphoreType.DMA,
-            pltpu.SemaphoreType.DMA,
-            pltpu.SemaphoreType.DMA,
-            pltpu.SemaphoreType.DMA,
-            pltpu.SemaphoreType.DMA,
-        ],
+        ]
+        + [pltpu.SemaphoreType.DMA] * 7
+        + cin_scratch(fields),
         compiler_params=pltpu.CompilerParams(
             collective_id=0, has_side_effects=True, vmem_limit_bytes=56 << 20
         ),
         name="step",
-    )(inv, target.reshape(1, -1), grads.reshape(samples * padded, width), numbers, table,
-      accum.reshape(rows_dev // 128, 128))
-    return new_table, new_accum.reshape(rows_dev), answers
-
-
-def pick_kernel(index_ref, rows_ref, out_ref):
-    def gather(k, carry):
+    )(inv, unique_ids, next_ids, table, accum.reshape(rows_dev // 128, 128), *operands)
+
+
+PIECES = 4
+
+
+def finish_kernel(starts_ref, answers_ref, nt_ref, na_ref, out_ref, nt_out, na_out, answers, table, lines, sem, ins, outs):
+    fetch = pltpu.make_async_copy(answers_ref, answers, sem)
+    fetch.start()
+    size = table.shape[0] // PIECES
+    pieces = [pl.ds(k * size, size) for k in range(PIECES)]
+    for k, at in enumerate(pieces):
+        pltpu.make_async_copy(nt_ref.at[at], table.at[at], ins.at[k]).start()
+    na_out[...] = na_ref[...]
+    fetch.wait()
+    for k, at in enumerate(pieces):
+        pltpu.make_async_copy(nt_ref.at[at], table.at[at], ins.at[k]).wait()
+        pltpu.make_async_copy(table.at[at], nt_out.at[at], outs.at[k]).start()
+
+    def place(k, carry):
         for t in range(8):
-            out_ref[pl.ds(k * 8 + t, 1), :] = rows_ref[pl.ds(index_ref[k * 8 + t], 1), :]
+            o = k * 8 + t
+            lines[pl.ds(starts_ref[o], RCAP), :] = answers[o]
         return carry
 
-    lax.fori_loop(0, out_ref.shape[0] // 8, gather, 0)
-
-
-def pick(rows, index):
-    vmem = pl.BlockSpec(memory_space=pltpu.VMEM)
+    lax.fori_loop(0, answers.shape[0] // 8, place, 0)
+    out_ref[...] = lines[: out_ref.shape[0], :]
+    for k, at in enumerate(pieces):
+        pltpu.make_async_copy(table.at[at], nt_out.at[at], outs.at[k]).wait()
+
+
+def finish(starts, answers, new_table, new_accum, asked):
+    vmem, free = pl.BlockSpec(memory_space=pltpu.VMEM), pl.BlockSpec(memory_space=pl.ANY)
+    width = answers.shape[2]
     return pl.pallas_call(
-        pick_kernel,
-        in_specs=[pl.BlockSpec(memory_space=pltpu.SMEM), vmem],
-        out_specs=vmem,
-        out_shape=jax.ShapeDtypeStruct((index.shape[0], rows.shape[1]), F32),
-        compiler_params=pltpu.CompilerParams(vmem_limit_bytes=32 << 20),
-        name="pick",
-    )(index, rows)
+        finish_kernel,
+        in_specs=[pl.BlockSpec(memory_space=pltpu.SMEM), free, free, vmem],
+        out_specs=[vmem, free, vmem],
+        out_shape=[
+            jax.ShapeDtypeStruct((asked, width), F32),
+            jax.ShapeDtypeStruct(new_table.shape, F32),
+            jax.ShapeDtypeStruct(new_accum.shape, F32),
+        ],
+        scratch_shapes=[
+            pltpu.VMEM(answers.shape, F32),
+            pltpu.VMEM(new_table.shape, F32),
+            pltpu.VMEM((asked + RCAP, width), F32),
+            pltpu.SemaphoreType.DMA,
+            pltpu.SemaphoreType.DMA((PIECES,)),
+            pltpu.SemaphoreType.DMA((PIECES,)),
+        ],
+        compiler_params=pltpu.CompilerParams(vmem_limit_bytes=60 << 20),
+        name="finish",
+    )(starts, answers, new_table, new_accum)
 
 
 def local(
@@ -434,23 +480,13 @@
     accum,
     next_ids,
 ):
-    rows_dev, width = table.shape
     owners = lax.axis_size("group") * lax.axis_size("member")
-    owner, within, inside = ranks(unique_ids[0], CAP, rows_dev)
-    target = within * owners + owner
-    ask_owner, ask_within, ask_inside = ranks(next_ids[0], RCAP, rows_dev)
-    ask_target = ask_owner * RCAP + ask_within
-    numbers = jnp.concatenate(
-        [
-            by_owner(owner, within, inside, owners, CAP),
-            by_owner(ask_owner, ask_within, ask_inside, owners, RCAP),
-        ],
-        axis=1,
-    )
-    numbers = jnp.pad(numbers.astype(F32), ((0, 0), (0, width - CAP - RCAP)))
-    grads = cin(embeddings, cot_first, cot_second, cot_third, w_first, w_second, w_third)
-    new_table, new_accum, answers = step(grads, inverse, target, numbers, table, accum)
-    return (new_table, new_accum, pick(answers.reshape(-1, width), ask_target)[None])
+    operands = cin_operands(embeddings, cot_first, cot_second, cot_third, w_first, w_second, w_third)
+    new_table, new_accum, answers = step(inverse, unique_ids, next_ids, table, accum, operands)
+    firsts = jnp.arange(owners, dtype=jnp.int32)[:, None] * table.shape[0]
+    starts = jnp.sum((next_ids < firsts).astype(jnp.int32), axis=1)
+    returned, new_table, new_accum = finish(starts, answers, new_table, new_accum, next_ids.shape[1])
+    return (new_table, new_accum.reshape(accum.shape), returned[None])
 
 
 def solution(mesh):

time: 132 us -> 118 us (0.89)
  Pallas kernels: 111 us -> 102 us
  local copies, waits for them, and re-layouts: 17 us -> 12.3 us
    pallas_call x3 -> x2, Pallas kernels: 111 us -> 102 us  [the longest x1 97.6 us: step(): pl.pallas_call(step_kernel, in_specs=[vmem] * 3 + [pl.BlockSpec(memory_sp...]
    unnamed x32 -> x24, local copies, waits for them, and re-layouts: 9.61 us -> 2.07 us
    transpose x2, local copies, waits for them, and re-layouts: 0.67 us -> 2.61 us  [columns(): return jnp.transpose(cot.reshape(samples // 2, 2, HP), (0, 2, 1))]
where the time goes in v3:
time: 118 us
  Pallas kernels  102 us (86%)
  local copies, waits for them, and re-layouts  12.3 us (10%)
  other arithmetic  2.32 us (2%)
    pallas_call x1, Pallas kernels, step(): pl.pallas_call(step_kernel, in_specs=[vmem] * 3 + [pl.BlockSpec(memory_sp...  97.6 us
    pallas_call x1, Pallas kernels, finish(): pl.pallas_call(finish_kernel, in_specs=[pl.BlockSpec(memory_space=pltpu.S...  4.7 us
    transpose x2, local copies, waits for them, and re-layouts, columns(): return jnp.transpose(cot.reshape(samples // 2, 2, HP), (0, 2, 1))  2.61 us

profile of v3, /device:TPU:1, one launch (start us, length us, event | category | flops | bytes accessed | tf_op | source)
XLA Modules:
  0.0 118.1 jit_solution(17284243765981508464)
XLA Ops:
  0.6 0.0 copy-start
  0.6 1.1 convert_element_type.31
  1.7 0.2 fusion.2
  1.9 0.1 pad_convert_fusion
  2.0 0.1 subtract_convert_fusion
  2.1 0.0 copy-start.3
  2.1 0.1 pad_maximum_fusion
  2.2 1.1 copy.43
  3.2 0.1 copy-done.3
  3.3 1.6 %copy.46 = bf16[39,100,100]{2,1,0:T(8,128)(2,1)S(1)} copy(bf16[39,100,100]{1,0,2:T(8,128)(2,1)S(1)} %bitcast.39) | data formatting | bytes 1560000
  4.9 0.0 copy-start.4
  4.9 0.2 pad.39.clone
  5.2 1.7 %copy.44.w2f_ref = bf16[112,4368]{1,0:T(8,128)(2,1)} copy(bf16[112,4368]{0,1:T(8,128)(2,1)S(1)} %bitcast.30) | data formatting | bytes 1956864 | tf_op jit(solution)/shard_map/slice | solution.py:135
  6.9 0.1 copy.37
  7.1 0.3 fusion
  7.4 0.0 copy-start.2
  7.4 1.9 %copy.38 = f32[112,48,32]{1,0,2:T(8,128)} copy(f32[112,48,32]{0,2,1:T(8,128)S(1)} %fusion) | data formatting | bytes 1376256 | tf_op jit(solution)/shard_map/hij,nh->nij/dot_general | solution.py:131
  9.3 0.0 copy-done.2
  9.3 0.1 copy.45
  9.3 0.1 pad.38.clone
  9.5 0.0 copy-start.5
  9.5 1.0 copy.40
  10.4 0.0 copy-done.8
  10.5 1.3 %copy.35 = f32[16,2,112]{1,2,0:T(8,128)} copy(f32[16,2,112]{2,1,0:T(2,128)S(1)} %bitcast.40) | data formatting | bytes 28672 | tf_op jit(solution)/shard_map/transpose | solution.py:128
  11.8 0.0 copy-done.9
  11.8 1.3 %copy.36 = f32[16,2,112]{1,2,0:T(8,128)} copy(f32[16,2,112]{2,1,0:T(2,128)S(1)} %bitcast.41) | data formatting | bytes 28672 | tf_op jit(solution)/shard_map/transpose | solution.py:128
  13.1 0.1 copy.34
  13.2 0.8 pad.34.e_ref
  14.0 0.7 reshape.37.inv_ref
  14.7 97.6 %step.1 = (f32[4096,128]{1,0:T(8,128)}, f32[32,128]{1,0:T(8,128)}, f32[256,8,128]{2,1,0:T(8,128)}) custom-call(s32[1,1280]{1,0:T(1,128)} %reshape.37.inv_ref, s32[1,768]{1,0:T(1,128)} %ids_ref.1, s32[1,1536]{1,0:T(1,128)} %next_ref.1, f32[4096,128]{1,0:T(8,128)} %table_ref.1, f32[32,128]{1,0:T(8,128)} %bitcast.42, bf16[32,48,128]{2,1,0:T(8,128)(2,1)} %pad.34.e_ref, ...), custom_call_target="tpu_custom_call" | custom-call | tf_op jit(solution)/shard_map/step/pallas_call | solution.py:386
  112.4 0.9 convert_reduce_fusion.starts_ref
  113.3 4.7 %finish.1 = (f32[1536,128]{1,0:T(8,128)}, f32[4096,128]{1,0:T(8,128)}, f32[32,128]{1,0:T(8,128)}) custom-call(s32[256]{0:T(256)} %convert_reduce_fusion.starts_ref, f32[256,8,128]{2,1,0:T(8,128)} %get-tuple-element.9.answers_ref, f32[4096,128]{1,0:T(8,128)} %get-tuple-element.10.nt_ref, f32[32,128]{1,0:T(8,128)} %get-tuple-element.11.na_ref), custom_call_target="tpu_custom_call" | custom-call | tf_op jit(solution)/shard_map/finish/pallas_call | solution.py:447
  (16 shorter events, 0.1 us)
Async XLA Ops:
  0.6 6.4 %copy-start = (bf16[32,100]{1,0:T(8,128)(2,1)S(1)}, bf16[32,100]{1,0:T(8,128)(2,1)}, u32[]{:S(2)}) copy-start(bf16[32,100]{1,0:T(8,128)(2,1)} %param.15) | copy-start | bytes 19204
  2.1 1.3 %copy-start.3 = (bf16[100,100,39]{1,2,0:T(8,128)(2,1)S(1)}, bf16[100,100,39]{1,2,0:T(8,128)(2,1)}, u32[]{:S(2)}) copy-start(bf16[100,100,39]{1,2,0:T(8,128)(2,1)} %param.17) | copy-start | bytes 2340004
  4.9 2.0 %copy-start.4 = (bf16[100,100,39]{1,2,0:T(8,128)(2,1)S(1)}, bf16[100,100,39]{1,2,0:T(8,128)(2,1)}, u32[]{:S(2)}) copy-start(bf16[100,100,39]{1,2,0:T(8,128)(2,1)} %param.18) | copy-start | bytes 2340004
  5.2 1.9 %copy-start.1 = (bf16[39,112,128]{2,1,0:T(8,128)(2,1)}, bf16[39,112,128]{2,1,0:T(8,128)(2,1)S(1)}, u32[]{:S(2)}) copy-start(bf16[39,112,128]{2,1,0:T(8,128)(2,1)S(1)} %pad.39.clone) | copy-start | bytes 3354628
  7.4 1.9 %copy-start.2 = (bf16[100,39,39]{0,2,1:T(8,128)(2,1)S(1)}, bf16[100,39,39]{0,2,1:T(8,128)(2,1)}, u32[]{:S(2)}) copy-start(bf16[100,39,39]{0,2,1:T(8,128)(2,1)} %param.16) | copy-start | bytes 912604
  9.3 1.2 copy-start.8
  9.3 2.5 %copy-start.9 = (bf16[32,100]{1,0:T(8,128)(2,1)S(1)}, bf16[32,100]{1,0:T(8,128)(2,1)}, u32[]{:S(2)}) copy-start(bf16[32,100]{1,0:T(8,128)(2,1)} %param.14) | copy-start | bytes 19204
  9.5 3.6 %copy-start.5 = (bf16[32,39,128]{2,0,1:T(8,128)(2,1)S(1)}, bf16[32,39,128]{2,0,1:T(8,128)(2,1)}, u32[]{:S(2)}) copy-start(bf16[32,39,128]{2,0,1:T(8,128)(2,1)} %param.12) | copy-start | bytes 958468
  10.4 3.6 %copy-start.7 = (s32[32,39]{1,0:T(8,128)S(1)}, s32[32,39]{1,0:T(8,128)}, u32[]{:S(2)}) copy-start(s32[32,39]{1,0:T(8,128)} %param.20) | copy-start | bytes 14980
  14.7 97.6 %copy-start.6 = (s32[1,1536]{1,0:T(1,128)S(1)}, s32[1,1536]{1,0:T(1,128)}, u32[]{:S(2)}) copy-start(s32[1,1536]{1,0:T(1,128)} %next_ref.1) | copy-start | bytes 18436

commit v4 on v3

v4 whole, which is shorter than its diff:
```python
import jax
import jax.numpy as jnp
from jax import lax
from jax.experimental import pallas as pl
from jax.experimental.pallas import tpu as pltpu
from jax.sharding import PartitionSpec as P

FIELDS = 39
CAP = 4
RCAP = 8
RATE = 0.5
EPS = 1e-08

BF = jnp.bfloat16
F32 = jnp.float32


def halves(x):
    hi = x.astype(BF)
    return hi, (x - hi.astype(F32)).astype(BF)


def dot(a, b):
    return jnp.dot(a, b, preferred_element_type=F32)


FP = 48
FQ = 40
HP = 112
HQ = 104
KP = 128
JC = 3
LANES = 256


def half(s):
    return slice(s * 128, (s + 1) * 128)


def cin_layouts(e_ref, c1_ref, c2_ref, w1t_ref, w2b_ref, wide, columns, w1f, w2f):
    fields, samples = e_ref.shape[0], e_ref.shape[1]
    for f in range(fields):
        wide[f * samples : (f + 1) * samples, :] = e_ref[f].astype(F32)
    wide[fields * samples :, :] = jnp.zeros((wide.shape[0] - fields * samples, 128), F32)
    for k, ref in enumerate((c1_ref, c2_ref)):
        columns[k * HP : (k + 1) * HP, :] = ref[...].astype(F32).T[:HP].astype(BF)
    for source, to in ((w1t_ref, w1f), (w2b_ref, w2f)):

        def turn(c, carry, source=source, to=to):
            at = pl.ds(pl.multiple_of(c * 128, 128), 128)
            to[:, at] = source[at, :].astype(F32).T[:HP].astype(BF)
            return carry

        lax.fori_loop(0, source.shape[0] // 128, turn, 0, unroll=5)


def cin_first(g, top_ref, w2b_ref, wide, columns, w1f, w2f, keep, p1, p2, l1f, mid, l2s, fill):
    ef, part, low, base = keep
    fields, samples = FIELDS, columns.shape[1]
    for s in range(2):
        ef[:, half(s)] = wide[pl.ds(2 * g + s, FQ, stride=samples), :]
    e = jnp.concatenate([ef[...], jnp.zeros((FP - FQ, LANES), F32)], axis=0).astype(BF)
    e3 = e.reshape(FP // 16, 16, LANES)

    def row16(i):
        return jnp.broadcast_to(ef[i : i + 1, :], (16, LANES)).astype(BF)

    chosen = lax.broadcasted_iota(jnp.int32, (samples, LANES), 0) - 2 * g
    chosen = chosen == lax.broadcasted_iota(jnp.int32, (samples, LANES), 1) // 128
    cots = dot(columns[...], jnp.where(chosen, 1.0, 0.0).astype(BF))
    next(fill, None)
    uppers = []
    for s in range(2):
        top, one = top_ref[2 * g + s].T, e[:, half(s)]
        hi, lo = halves(top)
        rest = (top - hi.astype(F32) - lo.astype(F32)).astype(BF)
        grad_two = dot(hi, one) + (dot(lo, one) + dot(rest, one))
        uppers.append((cots[HP:, half(s)] + grad_two).astype(BF))
    upper = jnp.concatenate(uppers, axis=1)
    upper = jnp.concatenate([upper, jnp.zeros((KP - HP, LANES), BF)], axis=0)
    next(fill, None)
    for i in range(fields):
        p1[i * FP : (i + 1) * FP, :] = (e3 * row16(i)[None]).reshape(FP, LANES)
        if i % 13 == 12:
            next(fill, None)
    l1 = dot(w1f[:, : fields * FP], p1[...]).astype(BF)
    l1f[...] = l1.astype(F32)
    l3 = l1.reshape(HP // 16, 16, LANES)
    for _ in fill:
        pass

    acc = [jnp.zeros((HQ // 8, 8, 128), F32) for _ in range(2)]
    done = 0
    for c in range(fields // JC):
        mid[c % 2] = dot(w2b_ref[c * JC * HP : (c + 1) * JC * HP, :], upper)
        for k in range(JC):
            j = c * JC + k
            p2[j * HP : (j + 1) * HP, :] = (l3 * row16(j)[None]).reshape(HP, LANES)
        ready = (c + 1) * JC * HP
        if c + 1 < fields // JC:
            ready = ready // 512 * 512
        if ready > done:
            piece = dot(w2f[:, done:ready], p2[done:ready, :])
            if done:
                piece = piece + l2s[...]
            l2s[...] = piece
            done = ready
        for s in range(2):
            one = l1f[:HQ, half(s)].reshape(HQ // 8, 8, 128)
            for k in range(JC):
                j = c * JC + k
                m = mid[c % 2, k * HP : k * HP + HQ, half(s)].reshape(HQ // 8, 8, 128)
                b = jnp.broadcast_to(ef[j : j + 1, half(s)], (8, 128))
                acc[s] = acc[s] + m * b[None]
                part[j, :, half(s)] = jnp.sum(m * one, axis=0)
    part[fields:, :, :] = jnp.zeros((FQ - fields, 8, LANES), F32)
    l2 = l2s[...].astype(BF)
    lower = jnp.concatenate([acc[s].reshape(HQ, 128) for s in range(2)], axis=1)
    lower = (cots[:HQ] + lower).astype(F32)
    low[...] = jnp.concatenate([lower, jnp.zeros((KP - HQ, LANES), F32)], axis=0).astype(BF)
    for s in range(2):
        hi, lo = halves(top_ref[2 * g + s])
        base[:, half(s)] = dot(hi, l2[:, half(s)]) + dot(lo, l2[:, half(s)])


def cin_last(g, w1b_ref, out_ref, keep, bot):
    ef, part, low, base = keep
    blocks = FQ // 8
    lower = jnp.concatenate([low[...], low[...]], axis=0)
    sums = [[base[8 * i : 8 * i + 8, half(s)] for i in range(blocks)] for s in range(2)]
    at = 0
    for b in range(blocks):
        rows = 8 * (b + 1)
        product = dot(w1b_ref[at : at + 8 * rows, :], lower)
        bot[b % 2, : 8 * rows, :] = product
        at += 8 * rows
        for s in range(2):
            es = ef[:rows, half(s)].reshape(b + 1, 8, 128)
            for k in range(8):
                j = b * 8 + k
                m = bot[b % 2, k * rows : (k + 1) * rows, half(s)].reshape(b + 1, 8, 128)
                part[j, :, half(s)] = part[j, :, half(s)] + jnp.sum(m * es, axis=0)
                one = jnp.broadcast_to(ef[j : j + 1, half(s)], (8, 128))
                for i in range(b):
                    sums[s][i] = sums[s][i] + m[i] * one
        yield
    for s in range(2):
        out_ref[2 * g + s] = jnp.sum(part[:, :, half(s)], axis=1) + jnp.concatenate(sums[s], axis=0)
        yield


def cin_all(
    between,
    e_ref, c1_ref, c2_ref, top_ref, w1t_ref, w2b_ref, w1b_ref, out_ref,
    wide, columns, w1f, w2f, p1, p2, l1f, mid, l2s, bot, *kept,
):
    keeps = (kept[:4], kept[4:])
    cin_layouts(e_ref, c1_ref, c2_ref, w1t_ref, w2b_ref, wide, columns, w1f, w2f)
    turns = columns.shape[1] // 4

    def turn(t, carry):
        between(t, turns)
        for k in range(2):
            g = 2 * t + k
            fill = cin_last(jnp.maximum(g - 1, 0), w1b_ref, out_ref, keeps[1 - k], bot)
            cin_first(
                g, top_ref, w2b_ref, wide, columns, w1f, w2f, keeps[k], p1, p2, l1f, mid, l2s, fill
            )
        return carry

    lax.fori_loop(0, turns, turn, 0)
    for _ in cin_last(2 * turns - 1, w1b_ref, out_ref, keeps[1], bot):
        pass


def cin_operands(embeddings, cot_first, cot_second, cot_third, w_first, w_second, w_third):
    maps, fields = w_first.shape[:2]
    e = jnp.transpose(embeddings, (1, 0, 2))

    def wide(cot):
        return jnp.pad(cot, ((0, 0), (0, KP - maps)))

    w_third = jnp.pad(w_third, ((0, 0), (0, HP - maps), (0, FP - fields)))
    top = jnp.einsum("hij,nh->nji", w_third, cot_third, preferred_element_type=F32)

    w2b = jnp.transpose(w_second, (2, 1, 0))
    w2b = jnp.pad(w2b, ((0, FQ - fields), (0, HP - maps), (0, KP - maps))).reshape(FQ * HP, KP)
    w1 = jnp.transpose(w_first, (1, 2, 0))
    w1t = jnp.pad(w1, ((0, FQ - fields), (0, FP - fields), (0, KP - maps))).reshape(FQ * FP, KP)
    both = w1.astype(F32)
    both = both + jnp.swapaxes(both, 0, 1)
    both = jnp.pad(both, ((0, FQ - fields), (0, FQ - fields), (0, KP - maps)))
    both = [both[8 * b : 8 * b + 8, : 8 * (b + 1)].reshape(-1, KP) for b in range(FQ // 8)]
    w1b = jnp.concatenate(halves(jnp.concatenate(both, axis=0)), axis=1)
    return e, wide(cot_first), wide(cot_second), top, w1t, w2b, w1b


def cin_scratch(samples):
    return [
        pltpu.VMEM((FQ * samples, 128), F32),
        pltpu.VMEM((2 * HP, samples), BF),
        pltpu.VMEM((HP, FQ * FP), BF),
        pltpu.VMEM((HP, FQ * HP), BF),
        pltpu.VMEM((FIELDS * FP, LANES), BF),
        pltpu.VMEM((FIELDS * HP, LANES), BF),
        pltpu.VMEM((HP, LANES), F32),
        pltpu.VMEM((2, JC * HP, LANES), F32),
        pltpu.VMEM((HP, LANES), F32),
        pltpu.VMEM((2, 8 * FQ, LANES), F32),
    ] + [
        pltpu.VMEM((FQ, LANES), F32),
        pltpu.VMEM((FQ, 8, LANES), F32),
        pltpu.VMEM((KP, LANES), BF),
        pltpu.VMEM((FP, LANES), F32),
    ] * 2


def ranks(row_list, capacity, rows_dev):
    owner = row_list // rows_dev
    lane = lax.broadcasted_iota(jnp.int32, owner.shape, 1)
    within = jnp.zeros_like(owner)
    for k in range(1, capacity):
        same = jnp.logical_and(pltpu.roll(owner, k, 1) == owner, lane >= k)
        within = within + jnp.where(same, 1, 0)
    return owner, within, row_list - owner * rows_dev


def by_owner(owner, within, inside, owners, capacity):
    hot = lax.broadcasted_iota(jnp.int32, (owners, owner.shape[1]), 0) == owner
    hot = jnp.where(hot, 1.0, 0.0).astype(BF)
    place = lax.broadcasted_iota(jnp.int32, (8, owner.shape[1]), 0)
    value = jnp.where(place == within, inside + 1, 0)
    high = value // 64
    value = jnp.concatenate([high.astype(F32), (value - high * 64).astype(F32)], axis=0).astype(BF)
    found = lax.dot_general(hot, value, (((1,), (1,)), ((), ())), preferred_element_type=F32)
    return found[:, :8] * 64 + found[:, 8:] - 1


MESH = pl.DeviceIdType.MESH
CLASSES = 4


def outward(k, middle):
    return middle + (1 - 2 * (k % 2)) * ((k + 1) // 2)


def moved(step):
    group, member = lax.axis_index("group"), lax.axis_index("member")
    x, z, core = member // 16, (member // 2) % 8, member % 2
    group = (group + outward(step // 64, 2)) % 4
    z = (z + outward((step // 8) % 8, 4)) % 8
    x = (x + outward((step // 2) % 4, 2)) % 4
    return group, x * 16 + z * 2 + (core + step + 1) % 2


class Tree:
    def __init__(self):
        self.sem = pltpu.get_barrier_semaphore()
        self.group, member = lax.axis_index("group"), lax.axis_index("member")
        self.x, self.rest = member // 16, member % 16
        top = self.group * 4 + self.x
        self.root = jnp.logical_and(top == 0, self.rest == 0)
        self.leader = jnp.logical_and(top != 0, self.rest == 0)

    def signal(self, group, member):
        pl.semaphore_signal(self.sem, inc=1, device_id=(group, member), device_id_type=MESH)

    def arrive(self):
        @pl.when(self.rest != 0)
        def _():
            self.signal(self.group, self.x * 16)

    def pass_up(self):
        @pl.when(self.leader)
        def _():
            pl.semaphore_wait(self.sem, 15)
            self.signal(0, 0)

    def turn(self):
        @pl.when(self.root)
        def _():
            pl.semaphore_wait(self.sem, 30)

            def tell(k, carry):
                self.signal(k // 4, (k % 4) * 16)
                return carry

            lax.fori_loop(1, 16, tell, 0)

    def release(self):
        @pl.when(jnp.logical_not(self.root))
        def _():
            pl.semaphore_wait(self.sem, 1)

        @pl.when(self.rest == 0)
        def _():
            def tell(k, carry):
                self.signal(self.group, self.x * 16 + k)
                return carry

            lax.fori_loop(1, 16, tell, 0)


def step_kernel(
    inv_ref, ids_ref, next_ref, table_ref, accum_ref,
    e_ref, c1_ref, c2_ref, top_ref, w1t_ref, w2b_ref, w1b_ref,
    nt_out, na_ref, answers_ref, starts_ref,
    nt_ref, hot, high, grad, grads, send, rows, found, ask_v, ask_s, rows_out, rows_in, answers_out, answers_in, own, table_in, table_out,
    *scratch,
):
    tree = Tree()
    tree.arrive()
    table_copy = pltpu.make_async_copy(table_ref, nt_ref, table_in)
    table_copy.start()
    grad[...] = jnp.zeros_like(grad)
    ask_v[...] = jnp.zeros_like(ask_v)
    owners, width = send.shape[0], send.shape[2]
    rows_dev = table_ref.shape[0]
    me = lax.axis_index("group") * 64 + lax.axis_index("member")
    count, listed = inv_ref.shape[1], ids_ref.shape[1]

    owner, within, inside = ranks(ids_ref[...], CAP, rows_dev)
    target = within * owners + owner
    ask_owner, ask_within, ask_inside = ranks(next_ref[...], RCAP, rows_dev)
    numbers = [
        by_owner(owner, within, inside, owners, CAP),
        by_owner(ask_owner, ask_within, ask_inside, owners, RCAP),
    ]
    send[:, CAP, :] = jnp.concatenate(numbers + [jnp.zeros((owners, width - 16), F32)], axis=1)
    before = ask_owner < lax.broadcasted_iota(jnp.int32, (owners, ask_owner.shape[1]), 0)
    starts = lax.dot_general(
        jnp.ones((16, ask_owner.shape[1]), BF), jnp.where(before, 1.0, 0.0).astype(BF),
        (((1,), (1,)), ((), ())), preferred_element_type=F32,
    )
    starts_ref[...] = starts[:8].astype(jnp.int32)

    def between(turn, turns):
        pl.when(turn == turns // 4)(tree.pass_up)
        pl.when(turn == turns // 2)(tree.turn)
        pl.when(turn == turns * 3 // 4)(tree.release)

    cin_all(
        between, e_ref, c1_ref, c2_ref, top_ref, w1t_ref, w2b_ref, w1b_ref, grads, *scratch
    )

    g = jnp.concatenate(halves(grads[...].reshape(count, width)), axis=1)
    merged = []
    for b in range(listed // 256):
        place = lax.broadcasted_iota(jnp.int32, (256, count), 0) + b * 256
        m = dot(jnp.where(place == inv_ref[...], 1.0, 0.0).astype(BF), g)
        merged.append(m[:, :width] + m[:, width:])
    merged = jnp.concatenate(halves(jnp.concatenate(merged, axis=0)), axis=1)
    for c in range(CAP):
        place = lax.broadcasted_iota(jnp.int32, (owners, listed), 0) + c * owners
        m = dot(jnp.where(place == target, 1.0, 0.0).astype(BF), merged)
        send[:, c, :] = m[:, :width] + m[:, width:]
    rows[me] = send[me]

    def send_rows(k, carry):
        to, member = moved(k)
        pltpu.make_async_remote_copy(
            src_ref=send.at[to * 64 + member], dst_ref=rows.at[me],
            send_sem=rows_out, recv_sem=rows_in.at[k // 64],
            device_id=(to, member), device_id_type=MESH,
        ).start()
        return carry

    lax.fori_loop(0, owners - 1, send_rows, 0)

    part = owners // CLASSES
    group = lax.axis_index("group")

    def arrived(c, count):
        origin = (group - outward(c, 2) + CLASSES) % CLASSES
        at = pl.ds(pl.multiple_of(origin * part, part), count)
        pltpu.make_async_copy(send.at[at], rows.at[at], rows_in.at[c]).wait()
        at = pl.ds(pl.multiple_of(origin * part, part), part)
        numbers = rows[at, CAP, :].T[:16, :part].astype(jnp.int32)
        ask_v[origin, :, :part] = jnp.clip(numbers, 0, rows_dev - 1)
        values = jnp.concatenate([rows[at, k, :] for k in range(CAP)], axis=0)
        row = jnp.concatenate([numbers[k : k + 1] for k in range(CAP)], axis=1)
        place = lax.broadcasted_iota(jnp.int32, (64, CAP * part), 0)
        high[...] = jnp.where(place == row // 64, 1.0, 0.0)
        low = jnp.where(place == row - row // 64 * 64, 1.0, 0.0).astype(BF)
        return jnp.concatenate(halves(values), axis=1), low.reshape(4, 16, CAP * part)

    def product(b, values, low):
        for k in range(16):
            one = jnp.broadcast_to(high[pl.ds(b * 16 + k, 1), :], (16, CAP * part)).astype(BF)
            hot[k * 64 : (k + 1) * 64, :] = (low * one[None]).reshape(64, CAP * part)
        s = dot(hot[...], values)
        return s[:, :width] + s[:, width:]

    blocks = rows_dev // 1024

    def add_class(c, carry):
        values, low = arrived(c, part)

        def block(b, carry):
            at = pl.ds(pl.multiple_of(b * 1024, 1024), 1024)
            s = product(b, values, low)
            grad[at, :] = grad[at, :] + s
            return carry

        lax.fori_loop(0, blocks, block, 0)
        return carry

    lax.fori_loop(0, CLASSES - 1, add_class, 0)
    values, low = arrived(CLASSES - 1, part - 1)
    to_scalars = pltpu.make_async_copy(ask_v, ask_s, own)
    to_scalars.start()
    table_copy.wait()
    lane = lax.broadcasted_iota(jnp.int32, (128, 128), 1)

    def update(b, carry):
        at = pl.ds(pl.multiple_of(b * 1024, 1024), 1024)
        g = grad[at, :] + product(b, values, low)
        grad[at, :] = g
        total = dot(jnp.concatenate(halves(g * g), axis=1), jnp.ones((2 * width, 128), BF))
        means = jnp.zeros((128, 128), F32)
        for r in range(8):
            means = jnp.where(lane == r, total[r * 128 : (r + 1) * 128] * (1 / width), means)
        few = pl.ds(pl.multiple_of(8 * b, 8), 8)
        na = accum_ref[few, :] + means.T[:8]
        na_ref[few, :] = na
        scale = RATE / (jnp.sqrt(na) + EPS)
        scale = jnp.concatenate([scale, jnp.zeros((120, 128), F32)], axis=0).T
        for r in range(8):
            at = pl.ds(pl.multiple_of(b * 1024 + r * 128, 128), 128)
            nt_ref[at, :] = nt_ref[at, :] - grad[at, :] * scale[:, r : r + 1]
        return carry

    lax.fori_loop(0, blocks, update, 0)
    to_scalars.wait()

    def look_up(p):
        for t in range(RCAP):
            row = jnp.clip(ask_s[p // part, 8 + t, p % part], 0, rows_dev - 1)
            found[p, t : t + 1, :] = nt_ref[pl.ds(row, 1), :]

    late = 4

    def gather(k):
        to, member = moved(k)
        look_up(to * 64 + member)

    def send_answers(k):
        to, member = moved(k)
        pltpu.make_async_remote_copy(
            src_ref=found.at[to * 64 + member], dst_ref=answers_ref.at[me],
            send_sem=answers_out, recv_sem=answers_in,
            device_id=(to, member), device_id_type=MESH,
        ).start()

    def first(k, carry):
        gather(k)
        return carry

    def both(k, carry):
        gather(k)
        send_answers(k - late)
        return carry

    def last(k, carry):
        send_answers(k)
        return carry

    lax.fori_loop(0, late, first, 0)
    look_up(me)
    table_back = pltpu.make_async_copy(nt_ref, nt_out, table_out)
    table_back.start()
    lax.fori_loop(late, owners - 1, both, 0)
    mine = pltpu.make_async_copy(found.at[me], answers_ref.at[me], own)
    mine.start()
    lax.fori_loop(owners - 1 - late, owners - 1, last, 0)
    mine.wait()
    table_back.wait()
    others = pl.ds(0, owners - 1)
    pltpu.make_async_copy(send.at[others], rows.at[others], rows_out).wait()
    pltpu.make_async_copy(found.at[others], answers_ref.at[others], answers_in).wait()
    pltpu.make_async_copy(found.at[others], answers_ref.at[others], answers_out).wait()


def step(inverse, unique_ids, next_ids, table, accum, operands):
    rows_dev, width = table.shape
    samples, fields = inverse.shape
    owners = lax.axis_size("group") * lax.axis_size("member")
    count = samples * FQ
    inv = jnp.pad(inverse, ((0, 0), (0, FQ - fields)), constant_values=-1).reshape(1, -1)
    vmem = pl.BlockSpec(memory_space=pltpu.VMEM)
    return pl.pallas_call(
        step_kernel,
        in_specs=[vmem] * 3 + [pl.BlockSpec(memory_space=pl.ANY)] + [vmem] * (1 + len(operands)),
        out_specs=[pl.BlockSpec(memory_space=pl.ANY), vmem, pl.BlockSpec(memory_space=pl.ANY), vmem],
        out_shape=[
            jax.ShapeDtypeStruct(table.shape, F32),
            jax.ShapeDtypeStruct((rows_dev // 128, 128), F32),
            jax.ShapeDtypeStruct((owners, RCAP, width), F32),
            jax.ShapeDtypeStruct((8, owners), jnp.int32),
        ],
        scratch_shapes=[
            pltpu.VMEM(table.shape, F32),
            pltpu.VMEM((1024, CAP * owners // CLASSES), BF),
            pltpu.VMEM((64, CAP * owners // CLASSES), F32),
            pltpu.VMEM(table.shape, F32),
            pltpu.VMEM((samples, FQ, width), F32),
            pltpu.VMEM((owners, CAP + 1, width), F32),
            pltpu.VMEM((owners, CAP + 1, width), F32),
            pltpu.VMEM((owners, RCAP, width), F32),
            pltpu.VMEM((CLASSES, 16, 128), jnp.int32),
            pltpu.SMEM((CLASSES, 16, 128), jnp.int32),
            pltpu.SemaphoreType.DMA,
            pltpu.SemaphoreType.DMA((CLASSES,)),
        ]
        + [pltpu.SemaphoreType.DMA] * 5
        + cin_scratch(samples),
        compiler_params=pltpu.CompilerParams(
            collective_id=0, has_side_effects=True, vmem_limit_bytes=56 << 20
        ),
        name="step",
    )(inv, unique_ids, next_ids, table, accum.reshape(rows_dev // 128, 128), *operands)


PIECES = 4


def finish_kernel(starts_ref, answers_ref, nt_ref, na_ref, out_ref, nt_out, na_out, answers, table, lines, sems):
    some, size = answers.shape[0] // PIECES, table.shape[0] // PIECES

    def fetch(k):
        at = pl.ds(k * some, some)
        return pltpu.make_async_copy(answers_ref.at[at], answers.at[at], sems.at[0, k])

    def table_in(k):
        at = pl.ds(k * size, size)
        return pltpu.make_async_copy(nt_ref.at[at], table.at[at], sems.at[1, k])

    def table_out(k):
        at = pl.ds(k * size, size)
        return pltpu.make_async_copy(table.at[at], nt_out.at[at], sems.at[2, k])

    for k in range(PIECES):
        fetch(k).start()
    for k in range(PIECES):
        table_in(k).start()
    na_out[...] = na_ref[...]

    def place(k, carry):
        for t in range(8):
            o = k * 8 + t
            lines[pl.ds(starts_ref[0, o], RCAP), :] = answers[o]
        return carry

    for k in range(PIECES):
        fetch(k).wait()
        lax.fori_loop(k * some // 8, (k + 1) * some // 8, place, 0)
        if k:
            table_in(k - 1).wait()
            table_out(k - 1).start()
    table_in(PIECES - 1).wait()
    table_out(PIECES - 1).start()
    result = pltpu.make_async_copy(lines.at[pl.ds(0, out_ref.shape[0])], out_ref, sems.at[3, 0])
    result.start()
    for k in range(PIECES):
        table_out(k).wait()
    result.wait()


def finish(starts, answers, new_table, new_accum, asked):
    vmem, free = pl.BlockSpec(memory_space=pltpu.VMEM), pl.BlockSpec(memory_space=pl.ANY)
    width = answers.shape[2]
    return pl.pallas_call(
        finish_kernel,
        in_specs=[pl.BlockSpec(memory_space=pltpu.SMEM), free, free, vmem],
        out_specs=[free, free, vmem],
        out_shape=[
            jax.ShapeDtypeStruct((asked, width), F32),
            jax.ShapeDtypeStruct(new_table.shape, F32),
            jax.ShapeDtypeStruct(new_accum.shape, F32),
        ],
        scratch_shapes=[
            pltpu.VMEM(answers.shape, F32),
            pltpu.VMEM(new_table.shape, F32),
            pltpu.VMEM((asked + RCAP, width), F32),
            pltpu.SemaphoreType.DMA((4, PIECES)),
        ],
        compiler_params=pltpu.CompilerParams(vmem_limit_bytes=60 << 20),
        name="finish",
    )(starts, answers, new_table, new_accum)


def local(
    embeddings,
    cot_first,
    cot_second,
    cot_third,
    w_first,
    w_second,
    w_third,
    unique_ids,
    inverse,
    table,
    accum,
    next_ids,
):
    operands = cin_operands(embeddings, cot_first, cot_second, cot_third, w_first, w_second, w_third)
    new_table, new_accum, answers, starts = step(inverse, unique_ids, next_ids, table, accum, operands)
    returned, new_table, new_accum = finish(starts, answers, new_table, new_accum, next_ids.shape[1])
    return (new_table, new_accum.reshape(accum.shape), returned[None])


def solution(mesh):
    in_specs = (
        P(("group", "member"), None, None),
        P(("group", "member"), None),
        P(("group", "member"), None),
        P(("group", "member"), None),
        P(),
        P(),
        P(),
        P(("group", "member"), None),
        P(("group", "member"), None),
        P(("group", "member"), None),
        P(("group", "member")),
        P(("group", "member"), None),
    )
    out_specs = (
        P(("group", "member"), None),
        P(("group", "member")),
        P(("group", "member"), None, None),
    )
    return jax.shard_map(local, mesh=mesh, in_specs=in_specs, out_specs=out_specs, check_vma=False)
```

time: 118 us -> 128 us (1.085)
  Pallas kernels: 102 us -> 114 us
  local copies, waits for them, and re-layouts: 12.3 us -> 10.5 us
    pallas_call x1, Pallas kernels: 97.6 us -> 110 us  [step(): pl.pallas_call(step_kernel, in_specs=[vmem] * 3 + [pl.BlockSpec(memory_sp...]
    pad x3 -> x4, local copies, waits for them, and re-layouts: 1.15 us -> 5.68 us  [the longest x2 2.6 us: wide(): return jnp.pad(cot, ((0, 0), (0, KP - maps)))]
    transpose x2 -> x0, local copies, waits for them, and re-layouts: 2.61 us -> none  [columns(): return jnp.transpose(cot.reshape(samples // 2, 2, HP), (0, 2, 1))]
    slice x1 -> x9, local copies, waits for them, and re-layouts: 1.73 us -> 0.15 us  [cin_operands(): both[8 * b:8 * b + 8, :8 * (b + 1)].reshape(-1, KP)]
where the time goes in v4:
time: 128 us
  Pallas kernels  114 us (89%)
  local copies, waits for them, and re-layouts  10.5 us (8%)
  other arithmetic  2.09 us (2%)
    pallas_call x1, Pallas kernels, step(): pl.pallas_call(step_kernel, in_specs=[vmem] * 3 + [pl.BlockSpec(memory_sp...  110 us
    pallas_call x1, Pallas kernels, finish(): pl.pallas_call(finish_kernel, in_specs=[pl.BlockSpec(memory_space=pltpu.S...  4.47 us
    pad x2, local copies, waits for them, and re-layouts, wide(): return jnp.pad(cot, ((0, 0), (0, KP - maps)))  2.6 us

profile of v4, /device:TPU:1, one launch (start us, length us, event | category | flops | bytes accessed | tf_op | source)
XLA Modules:
  0.0 127.8 jit_solution(5595223228529060117)
XLA Ops:
  0.6 0.0 copy-start
  0.6 1.3 %pad.28.c1_ref = bf16[32,128]{1,0:T(8,128)(2,1)} pad(bf16[32,100]{1,0:T(8,128)(2,1)} %param.13, bf16[]{:T(256)} %constant.5.clone.1), padding=0_0x0_28 | pad | bytes 14594 | tf_op jit(solution)/shard_map/jit(_pad)/pad | solution.py:181
  2.0 1.3 %pad.29.c2_ref = bf16[32,128]{1,0:T(8,128)(2,1)} pad(bf16[32,100]{1,0:T(8,128)(2,1)} %param.14, bf16[]{:T(256)} %constant.5.clone.1), padding=0_0x0_28 | pad | bytes 14594 | tf_op jit(solution)/shard_map/jit(_pad)/pad | solution.py:181
  3.2 0.7 pad.27
  4.0 0.7 reshape.36.inv_ref
  4.7 1.9 %pad.31.clone = bf16[40,48,128]{2,1,0:T(8,128)(2,1)} pad(bf16[39,39,100]{2,1,0:T(8,128)(2,1)} %bitcast.27, bf16[]{:T(256)} %constant.5.clone.1), padding=0_1x0_9x0_28 | pad | bytes 795722 | tf_op jit(solution)/shard_map/jit(_pad)/pad | solution.py:189
  6.5 1.2 bitcast_add_fusion
  7.8 0.0 copy-start.1
  8.0 0.1 subtract_convert_fusion
  8.1 0.8 pad_maximum_fusion.w1b_ref
  8.9 0.1 copy-done.1
  9.0 0.0 copy-start.2
  9.0 1.6 %copy.26 = bf16[39,100,100]{2,1,0:T(8,128)(2,1)S(1)} copy(bf16[39,100,100]{1,0,2:T(8,128)(2,1)S(1)} %bitcast.28) | data formatting | bytes 1560000
  10.6 1.2 pad.32.clone
  11.9 0.0 copy-done.2
  11.9 0.1 copy.15
  12.0 0.0 copy-done
  12.0 0.3 fusion
  12.3 1.3 %copy.31 = f32[112,48,32]{0,1,2:T(8,128)} copy(f32[112,48,32]{0,2,1:T(8,128)S(1)} %fusion) | data formatting | bytes 1376256 | tf_op jit(solution)/shard_map/hij,nh->nji/dot_general | solution.py:184
  13.6 109.7 %step.1 = (f32[4096,128]{1,0:T(8,128)}, f32[32,128]{1,0:T(8,128)}, f32[256,8,128]{2,1,0:T(8,128)}, s32[8,256]{1,0:T(8,128)}) custom-call(s32[1,1280]{1,0:T(1,128)} %reshape.36.inv_ref, s32[1,768]{1,0:T(1,128)} %ids_ref.1, s32[1,1536]{1,0:T(1,128)} %next_ref.1, f32[4096,128]{1,0:T(8,128)} %table_ref.1, f32[32,128]{1,0:T(8,128)} %bitcast.34, ...), custom_call_target="tpu_custom_call" | custom-call | tf_op jit(solution)/shard_map/step/pallas_call | solution.py:491
  123.4 4.5 %finish.1 = (f32[1536,128]{1,0:T(8,128)}, f32[4096,128]{1,0:T(8,128)}, f32[32,128]{1,0:T(8,128)}) custom-call(s32[8,256]{1,0:T(8,128)} %get-tuple-element.10.starts_ref, f32[256,8,128]{2,1,0:T(8,128)} %get-tuple-element.11.answers_ref, f32[4096,128]{1,0:T(8,128)} %get-tuple-element.12.nt_ref, f32[32,128]{1,0:T(8,128)} %get-tuple-element.13.na_ref), custom_call_target="tpu_custom_call" | custom-call | tf_op jit(solution)/shard_map/finish/pallas_call | solution.py:572
  (14 shorter events, 0.2 us)
Async XLA Ops:
  0.6 11.4 %copy-start = (bf16[32,100]{1,0:T(8,128)(2,1)S(1)}, bf16[32,100]{1,0:T(8,128)(2,1)}, u32[]{:S(2)}) copy-start(bf16[32,100]{1,0:T(8,128)(2,1)} %param.15) | copy-start | bytes 19204
  7.8 1.2 copy-start.1
  9.0 2.8 %copy-start.2 = (bf16[100,100,39]{1,2,0:T(8,128)(2,1)S(1)}, bf16[100,100,39]{1,2,0:T(8,128)(2,1)}, u32[]{:S(2)}) copy-start(bf16[100,100,39]{1,2,0:T(8,128)(2,1)} %param.18) | copy-start | bytes 2340004

commit v5 on v4

--- a/solution.py
+++ b/solution.py
@@ -37,14 +37,20 @@
     return slice(s * 128, (s + 1) * 128)
 
 
-def cin_layouts(e_ref, c1_ref, c2_ref, w1t_ref, w2b_ref, wide, columns, w1f, w2f):
+def cin_layouts(e_ref, c1_ref, c2_ref, w1_ref, w2_ref, wide, columns, tops, w1t, w2b, w1f, w2f):
     fields, samples = e_ref.shape[0], e_ref.shape[1]
+    maps = c1_ref.shape[1]
+    for ref in (columns, tops, w1t, w2b):
+        ref[...] = jnp.zeros_like(ref)
+    for f in range(fields):
+        w1t[f * FP : f * FP + fields, :maps] = w1_ref[f]
+        w2b[f * HP : f * HP + maps, :maps] = w2_ref[f]
     for f in range(fields):
         wide[f * samples : (f + 1) * samples, :] = e_ref[f].astype(F32)
     wide[fields * samples :, :] = jnp.zeros((wide.shape[0] - fields * samples, 128), F32)
     for k, ref in enumerate((c1_ref, c2_ref)):
-        columns[k * HP : (k + 1) * HP, :] = ref[...].astype(F32).T[:HP].astype(BF)
-    for source, to in ((w1t_ref, w1f), (w2b_ref, w2f)):
+        columns[k * HP : k * HP + maps, :] = ref[...].astype(F32).T.astype(BF)
+    for source, to in ((w1t, w1f), (w2b, w2f)):
 
         def turn(c, carry, source=source, to=to):
             at = pl.ds(pl.multiple_of(c * 128, 128), 128)
@@ -54,7 +60,7 @@
         lax.fori_loop(0, source.shape[0] // 128, turn, 0, unroll=5)
 
 
-def cin_first(g, top_ref, w2b_ref, wide, columns, w1f, w2f, keep, p1, p2, l1f, mid, l2s, fill):
+def cin_first(g, top_ref, w2b_ref, wide, columns, tops, w1f, w2f, keep, p1, p2, l1f, mid, l2s, fill):
     ef, part, low, base = keep
     fields, samples = FIELDS, columns.shape[1]
     for s in range(2):
@@ -71,7 +77,8 @@
     next(fill, None)
     uppers = []
     for s in range(2):
-        top, one = top_ref[2 * g + s].T, e[:, half(s)]
+        tops[s, :fields, : top_ref.shape[2]] = top_ref[2 * g + s]
+        top, one = tops[s].T[:HP], e[:, half(s)]
         hi, lo = halves(top)
         rest = (top - hi.astype(F32) - lo.astype(F32)).astype(BF)
         grad_two = dot(hi, one) + (dot(lo, one) + dot(rest, one))
@@ -119,7 +126,7 @@
     lower = (cots[:HQ] + lower).astype(F32)
     low[...] = jnp.concatenate([lower, jnp.zeros((KP - HQ, LANES), F32)], axis=0).astype(BF)
     for s in range(2):
-        hi, lo = halves(top_ref[2 * g + s])
+        hi, lo = halves(tops[s][:, :HP])
         base[:, half(s)] = dot(hi, l2[:, half(s)]) + dot(lo, l2[:, half(s)])
 
 
@@ -151,11 +158,11 @@
 
 def cin_all(
     between,
-    e_ref, c1_ref, c2_ref, top_ref, w1t_ref, w2b_ref, w1b_ref, out_ref,
-    wide, columns, w1f, w2f, p1, p2, l1f, mid, l2s, bot, *kept,
+    e_ref, c1_ref, c2_ref, top_ref, w1_ref, w2_ref, w1b_ref, out_ref,
+    wide, columns, tops, w1t, w2b, w1f, w2f, p1, p2, l1f, mid, l2s, bot, *kept,
 ):
     keeps = (kept[:4], kept[4:])
-    cin_layouts(e_ref, c1_ref, c2_ref, w1t_ref, w2b_ref, wide, columns, w1f, w2f)
+    cin_layouts(e_ref, c1_ref, c2_ref, w1_ref, w2_ref, wide, columns, tops, w1t, w2b, w1f, w2f)
     turns = columns.shape[1] // 4
 
     def turn(t, carry):
@@ -164,7 +171,7 @@
             g = 2 * t + k
             fill = cin_last(jnp.maximum(g - 1, 0), w1b_ref, out_ref, keeps[1 - k], bot)
             cin_first(
-                g, top_ref, w2b_ref, wide, columns, w1f, w2f, keeps[k], p1, p2, l1f, mid, l2s, fill
+                g, top_ref, w2b, wide, columns, tops, w1f, w2f, keeps[k], p1, p2, l1f, mid, l2s, fill
             )
         return carry
 
@@ -177,28 +184,24 @@
     maps, fields = w_first.shape[:2]
     e = jnp.transpose(embeddings, (1, 0, 2))
 
-    def wide(cot):
-        return jnp.pad(cot, ((0, 0), (0, KP - maps)))
-
-    w_third = jnp.pad(w_third, ((0, 0), (0, HP - maps), (0, FP - fields)))
     top = jnp.einsum("hij,nh->nji", w_third, cot_third, preferred_element_type=F32)
-
-    w2b = jnp.transpose(w_second, (2, 1, 0))
-    w2b = jnp.pad(w2b, ((0, FQ - fields), (0, HP - maps), (0, KP - maps))).reshape(FQ * HP, KP)
+    w2 = jnp.transpose(w_second, (2, 1, 0))
     w1 = jnp.transpose(w_first, (1, 2, 0))
-    w1t = jnp.pad(w1, ((0, FQ - fields), (0, FP - fields), (0, KP - maps))).reshape(FQ * FP, KP)
     both = w1.astype(F32)
     both = both + jnp.swapaxes(both, 0, 1)
     both = jnp.pad(both, ((0, FQ - fields), (0, FQ - fields), (0, KP - maps)))
     both = [both[8 * b : 8 * b + 8, : 8 * (b + 1)].reshape(-1, KP) for b in range(FQ // 8)]
     w1b = jnp.concatenate(halves(jnp.concatenate(both, axis=0)), axis=1)
-    return e, wide(cot_first), wide(cot_second), top, w1t, w2b, w1b
+    return e, cot_first, cot_second, top, w1, w2, w1b
 
 
 def cin_scratch(samples):
     return [
         pltpu.VMEM((FQ * samples, 128), F32),
         pltpu.VMEM((2 * HP, samples), BF),
+        pltpu.VMEM((2, FP, 128), F32),
+        pltpu.VMEM((FQ * FP, KP), BF),
+        pltpu.VMEM((FQ * HP, KP), BF),
         pltpu.VMEM((HP, FQ * FP), BF),
         pltpu.VMEM((HP, FQ * HP), BF),
         pltpu.VMEM((FIELDS * FP, LANES), BF),
@@ -244,13 +247,19 @@
     return middle + (1 - 2 * (k % 2)) * ((k + 1) // 2)
 
 
-def moved(step):
-    group, member = lax.axis_index("group"), lax.axis_index("member")
-    x, z, core = member // 16, (member // 2) % 8, member % 2
-    group = (group + outward(step // 64, 2)) % 4
-    z = (z + outward((step // 8) % 8, 4)) % 8
-    x = (x + outward((step // 2) % 4, 2)) % 4
-    return group, x * 16 + z * 2 + (core + step + 1) % 2
+class Peers:
+    def __init__(self):
+        self.group, member = lax.axis_index("group"), lax.axis_index("member")
+        x, self.z, core = member // 16, (member // 2) % 8, member % 2
+        self.near = [
+            ((x + dx) % 4) * 16 + (core + dc) % 2 for dx in (2, 1, 3, 0) for dc in (1, 0)
+        ]
+        self.steps = 32
+
+    def at(self, step):
+        to = (self.group + outward(step // 8, 2)) % 4
+        first = ((self.z + outward(step % 8, 4)) % 8) * 2
+        return to, [first + n for n in self.near]
 
 
 class Tree:
@@ -303,7 +312,7 @@
 
 def step_kernel(
     inv_ref, ids_ref, next_ref, table_ref, accum_ref,
-    e_ref, c1_ref, c2_ref, top_ref, w1t_ref, w2b_ref, w1b_ref,
+    e_ref, c1_ref, c2_ref, top_ref, w1_ref, w2_ref, w1b_ref,
     nt_out, na_ref, answers_ref, starts_ref,
     nt_ref, hot, high, grad, grads, send, rows, found, ask_v, ask_s, rows_out, rows_in, answers_out, answers_in, own, table_in, table_out,
     *scratch,
@@ -340,7 +349,7 @@
         pl.when(turn == turns * 3 // 4)(tree.release)
 
     cin_all(
-        between, e_ref, c1_ref, c2_ref, top_ref, w1t_ref, w2b_ref, w1b_ref, grads, *scratch
+        between, e_ref, c1_ref, c2_ref, top_ref, w1_ref, w2_ref, w1b_ref, grads, *scratch
     )
 
     g = jnp.concatenate(halves(grads[...].reshape(count, width)), axis=1)
@@ -356,16 +365,19 @@
         send[:, c, :] = m[:, :width] + m[:, width:]
     rows[me] = send[me]
 
-    def send_rows(k, carry):
-        to, member = moved(k)
-        pltpu.make_async_remote_copy(
-            src_ref=send.at[to * 64 + member], dst_ref=rows.at[me],
-            send_sem=rows_out, recv_sem=rows_in.at[k // 64],
-            device_id=(to, member), device_id_type=MESH,
-        ).start()
-        return carry
-
-    lax.fori_loop(0, owners - 1, send_rows, 0)
+    peers = Peers()
+
+    def send_rows(step, count=8):
+        to, members = peers.at(step)
+        for member in members[:count]:
+            pltpu.make_async_remote_copy(
+                src_ref=send.at[to * 64 + member], dst_ref=rows.at[me],
+                send_sem=rows_out, recv_sem=rows_in.at[step // 8],
+                device_id=(to, member), device_id_type=MESH,
+            ).start()
+
+    lax.fori_loop(0, peers.steps - 1, lambda step, carry: (send_rows(step), carry)[1], 0)
+    send_rows(peers.steps - 1, 7)
 
     part = owners // CLASSES
     group = lax.axis_index("group")
@@ -433,46 +445,35 @@
     lax.fori_loop(0, blocks, update, 0)
     to_scalars.wait()
 
-    def look_up(p):
-        for t in range(RCAP):
-            row = jnp.clip(ask_s[p // part, 8 + t, p % part], 0, rows_dev - 1)
-            found[p, t : t + 1, :] = nt_ref[pl.ds(row, 1), :]
-
-    late = 4
-
-    def gather(k):
-        to, member = moved(k)
-        look_up(to * 64 + member)
-
-    def send_answers(k):
-        to, member = moved(k)
-        pltpu.make_async_remote_copy(
-            src_ref=found.at[to * 64 + member], dst_ref=answers_ref.at[me],
-            send_sem=answers_out, recv_sem=answers_in,
-            device_id=(to, member), device_id_type=MESH,
-        ).start()
-
-    def first(k, carry):
-        gather(k)
+    def gather(step):
+        to, members = peers.at(step)
+        for member in members:
+            for t in range(RCAP):
+                row = ask_s[to, 8 + t, member]
+                found[to * 64 + member, t : t + 1, :] = nt_ref[pl.ds(row, 1), :]
+
+    def send_answers(step, count=8):
+        to, members = peers.at(step)
+        for member in members[:count]:
+            pltpu.make_async_remote_copy(
+                src_ref=found.at[to * 64 + member], dst_ref=answers_ref.at[me],
+                send_sem=answers_out, recv_sem=answers_in,
+                device_id=(to, member), device_id_type=MESH,
+            ).start()
+
+    def both(step, carry):
+        gather(step)
+        send_answers(step - 1)
         return carry
 
-    def both(k, carry):
-        gather(k)
-        send_answers(k - late)
-        return carry
-
-    def last(k, carry):
-        send_answers(k)
-        return carry
-
-    lax.fori_loop(0, late, first, 0)
-    look_up(me)
+    gather(0)
+    lax.fori_loop(1, 4, both, 0)
     table_back = pltpu.make_async_copy(nt_ref, nt_out, table_out)
     table_back.start()
-    lax.fori_loop(late, owners - 1, both, 0)
+    lax.fori_loop(4, peers.steps, both, 0)
+    send_answers(peers.steps - 1, 7)
     mine = pltpu.make_async_copy(found.at[me], answers_ref.at[me], own)
     mine.start()
-    lax.fori_loop(owners - 1 - late, owners - 1, last, 0)
     mine.wait()
     table_back.wait()
     others = pl.ds(0, owners - 1)

time: 128 us -> 104 us (0.81)
  Pallas kernels: 114 us -> 96 us
  local copies, waits for them, and re-layouts: 10.5 us -> 5.03 us
    pallas_call x1, Pallas kernels: 110 us -> 91.5 us  [step(): pl.pallas_call(step_kernel, in_specs=[vmem] * 3 + [pl.BlockSpec(memory_sp...]
    pad x4 -> x0, local copies, waits for them, and re-layouts: 5.68 us -> none  [the longest x2 2.6 us: wide(): return jnp.pad(cot, ((0, 0), (0, KP - maps)))]
where the time goes in v5:
time: 104 us
  Pallas kernels  96 us (92%)
  local copies, waits for them, and re-layouts  5.03 us (5%)
    pallas_call x1, Pallas kernels, step(): pl.pallas_call(step_kernel, in_specs=[vmem] * 3 + [pl.BlockSpec(memory_sp...  91.5 us
    pallas_call x1, Pallas kernels, finish(): pl.pallas_call(finish_kernel, in_specs=[pl.BlockSpec(memory_space=pltpu.S...  4.47 us
    unnamed x11, local copies, waits for them, and re-layouts  2.24 us

profile of v5, /device:TPU:1, one launch (start us, length us, event | category | flops | bytes accessed | tf_op | source)
XLA Modules:
  0.0 103.7 jit_solution(5295753699968913963)
XLA Ops:
  0.6 0.0 copy-start
  0.6 0.0 copy-start.1
  0.7 0.8 pad.8
  1.5 0.7 reshape.30.inv_ref
  2.2 0.0 copy-done
  2.2 1.0 fusion
  3.2 1.2 %copy.23 = f32[32,100,39]{1,2,0:T(8,128)} copy(f32[32,100,39]{1,0,2:T(8,128)S(1)} %fusion) | data formatting | bytes 998400 | tf_op jit(solution)/shard_map/hij,nh->nji/dot_general | solution.py:187
  4.4 0.0 copy-done.1
  4.4 0.1 bitcast_add_fusion
  4.5 0.0 copy-start.2
  4.6 0.1 subtract_convert_fusion
  4.7 0.8 pad_maximum_fusion.w1b_ref
  5.5 0.4 copy-done.2
  5.9 1.8 %copy.17 = bf16[100,100,39]{0,1,2:T(8,128)(2,1)} copy(bf16[100,100,39]{1,2,0:T(8,128)(2,1)S(1)} %copy-done.2) | data formatting | bytes 1560000 | tf_op args[5]
  7.7 91.5 %step.1 = (f32[4096,128]{1,0:T(8,128)}, f32[32,128]{1,0:T(8,128)}, f32[256,8,128]{2,1,0:T(8,128)}, s32[8,256]{1,0:T(8,128)}) custom-call(s32[1,1280]{1,0:T(1,128)} %reshape.30.inv_ref, s32[1,768]{1,0:T(1,128)} %ids_ref.1, s32[1,1536]{1,0:T(1,128)} %next_ref.1, f32[4096,128]{1,0:T(8,128)} %table_ref.1, f32[32,128]{1,0:T(8,128)} %bitcast.31, ...), custom_call_target="tpu_custom_call" | custom-call | tf_op jit(solution)/shard_map/step/pallas_call | solution.py:492
  99.2 4.5 %finish.1 = (f32[1536,128]{1,0:T(8,128)}, f32[4096,128]{1,0:T(8,128)}, f32[32,128]{1,0:T(8,128)}) custom-call(s32[8,256]{1,0:T(8,128)} %get-tuple-element.10.starts_ref, f32[256,8,128]{2,1,0:T(8,128)} %get-tuple-element.11.answers_ref, f32[4096,128]{1,0:T(8,128)} %get-tuple-element.12.nt_ref, f32[32,128]{1,0:T(8,128)} %get-tuple-element.13.na_ref), custom_call_target="tpu_custom_call" | custom-call | tf_op jit(solution)/shard_map/finish/pallas_call | solution.py:573
  (9 shorter events, 0.1 us)
Async XLA Ops:
  0.6 1.5 %copy-start = (bf16[100,100,39]{1,2,0:T(8,128)(2,1)S(1)}, bf16[100,100,39]{1,2,0:T(8,128)(2,1)}, u32[]{:S(2)}) copy-start(bf16[100,100,39]{1,2,0:T(8,128)(2,1)} %param.18) | copy-start | bytes 2340004
  0.6 3.7 %copy-start.1 = (bf16[100,39,39]{0,2,1:T(8,128)(2,1)S(1)}, bf16[100,39,39]{0,2,1:T(8,128)(2,1)}, u32[]{:S(2)}) copy-start(bf16[100,39,39]{0,2,1:T(8,128)(2,1)} %param.16) | copy-start | bytes 912604
  4.5 1.4 %copy-start.2 = (bf16[100,100,39]{1,2,0:T(8,128)(2,1)S(1)}, bf16[100,100,39]{1,2,0:T(8,128)(2,1)}, u32[]{:S(2)}) copy-start(bf16[100,100,39]{1,2,0:T(8,128)(2,1)} %param.17) | copy-start | bytes 2340004

commit v6 on v5

--- a/solution.py
+++ b/solution.py
@@ -29,7 +29,7 @@
 HP = 112
 HQ = 104
 KP = 128
-JC = 3
+JC = 1
 LANES = 256
 
 
@@ -262,6 +262,21 @@
         return to, [first + n for n in self.near]
 
 
+def in_a_row(inverse, count):
+    samples, fields = inverse.shape
+    sample = (lax.broadcasted_iota(jnp.int32, (samples, count), 1) * 1639) // 65536
+    own = sample == lax.broadcasted_iota(jnp.int32, (samples, count), 0)
+    field = lax.broadcasted_iota(jnp.int32, (fields, count), 1)
+    field = field - (field * 1639) // 65536 * FQ
+    chosen = jnp.where(field == lax.broadcasted_iota(jnp.int32, (fields, count), 0), 1.0, 0.0).astype(BF)
+    value = inverse + 1
+    high = value // 64
+    both = jnp.concatenate([high.astype(F32), (value - high * 64).astype(F32)], axis=0).astype(BF)
+    spread = dot(both, chosen)
+    spread = jnp.where(own, spread[:samples] * 64 + spread[samples:], 0.0)
+    return jnp.sum(spread, axis=0, keepdims=True).astype(jnp.int32) - 1
+
+
 class Tree:
     def __init__(self):
         self.sem = pltpu.get_barrier_semaphore()
@@ -313,8 +328,8 @@
 def step_kernel(
     inv_ref, ids_ref, next_ref, table_ref, accum_ref,
     e_ref, c1_ref, c2_ref, top_ref, w1_ref, w2_ref, w1b_ref,
-    nt_out, na_ref, answers_ref, starts_ref,
-    nt_ref, hot, high, grad, grads, send, rows, found, ask_v, ask_s, rows_out, rows_in, answers_out, answers_in, own, table_in, table_out,
+    nt_ref, na_ref, answers_ref, starts_ref,
+    hot, high, grad, grads, send, rows, found, ask_v, ask_s, rows_out, rows_in, answers_out, answers_in, own, table_in,
     *scratch,
 ):
     tree = Tree()
@@ -326,7 +341,8 @@
     owners, width = send.shape[0], send.shape[2]
     rows_dev = table_ref.shape[0]
     me = lax.axis_index("group") * 64 + lax.axis_index("member")
-    count, listed = inv_ref.shape[1], ids_ref.shape[1]
+    count, listed = grads.shape[0] * FQ, ids_ref.shape[1]
+    positions = in_a_row(inv_ref[...], count)
 
     owner, within, inside = ranks(ids_ref[...], CAP, rows_dev)
     target = within * owners + owner
@@ -356,7 +372,7 @@
     merged = []
     for b in range(listed // 256):
         place = lax.broadcasted_iota(jnp.int32, (256, count), 0) + b * 256
-        m = dot(jnp.where(place == inv_ref[...], 1.0, 0.0).astype(BF), g)
+        m = dot(jnp.where(place == positions, 1.0, 0.0).astype(BF), g)
         merged.append(m[:, :width] + m[:, width:])
     merged = jnp.concatenate(halves(jnp.concatenate(merged, axis=0)), axis=1)
     for c in range(CAP):
@@ -414,7 +430,7 @@
             grad[at, :] = grad[at, :] + s
             return carry
 
-        lax.fori_loop(0, blocks, block, 0)
+        lax.fori_loop(0, blocks, block, 0, unroll=2)
         return carry
 
     lax.fori_loop(0, CLASSES - 1, add_class, 0)
@@ -442,7 +458,7 @@
             nt_ref[at, :] = nt_ref[at, :] - grad[at, :] * scale[:, r : r + 1]
         return carry
 
-    lax.fori_loop(0, blocks, update, 0)
+    lax.fori_loop(0, blocks, update, 0, unroll=True)
     to_scalars.wait()
 
     def gather(step):
@@ -467,15 +483,11 @@
         return carry
 
     gather(0)
-    lax.fori_loop(1, 4, both, 0)
-    table_back = pltpu.make_async_copy(nt_ref, nt_out, table_out)
-    table_back.start()
-    lax.fori_loop(4, peers.steps, both, 0)
+    lax.fori_loop(1, peers.steps, both, 0)
     send_answers(peers.steps - 1, 7)
     mine = pltpu.make_async_copy(found.at[me], answers_ref.at[me], own)
     mine.start()
     mine.wait()
-    table_back.wait()
     others = pl.ds(0, owners - 1)
     pltpu.make_async_copy(send.at[others], rows.at[others], rows_out).wait()
     pltpu.make_async_copy(found.at[others], answers_ref.at[others], answers_in).wait()
@@ -484,23 +496,20 @@
 
 def step(inverse, unique_ids, next_ids, table, accum, operands):
     rows_dev, width = table.shape
-    samples, fields = inverse.shape
+    samples = inverse.shape[0]
     owners = lax.axis_size("group") * lax.axis_size("member")
-    count = samples * FQ
-    inv = jnp.pad(inverse, ((0, 0), (0, FQ - fields)), constant_values=-1).reshape(1, -1)
     vmem = pl.BlockSpec(memory_space=pltpu.VMEM)
     return pl.pallas_call(
         step_kernel,
         in_specs=[vmem] * 3 + [pl.BlockSpec(memory_space=pl.ANY)] + [vmem] * (1 + len(operands)),
-        out_specs=[pl.BlockSpec(memory_space=pl.ANY), vmem, pl.BlockSpec(memory_space=pl.ANY), vmem],
+        out_specs=[vmem, vmem, vmem, vmem],
         out_shape=[
-            jax.ShapeDtypeStruct(table.shape, F32),
-            jax.ShapeDtypeStruct((rows_dev // 128, 128), F32),
-            jax.ShapeDtypeStruct((owners, RCAP, width), F32),
-            jax.ShapeDtypeStruct((8, owners), jnp.int32),
+            pltpu.VMEM(table.shape, F32),
+            pltpu.VMEM((rows_dev // 128, 128), F32),
+            pltpu.VMEM((owners, RCAP, width), F32),
+            pltpu.VMEM((8, owners), jnp.int32),
         ],
         scratch_shapes=[
-            pltpu.VMEM(table.shape, F32),
             pltpu.VMEM((1024, CAP * owners // CLASSES), BF),
             pltpu.VMEM((64, CAP * owners // CLASSES), F32),
             pltpu.VMEM(table.shape, F32),
@@ -513,57 +522,33 @@
             pltpu.SemaphoreType.DMA,
             pltpu.SemaphoreType.DMA((CLASSES,)),
         ]
-        + [pltpu.SemaphoreType.DMA] * 5
+        + [pltpu.SemaphoreType.DMA] * 4
         + cin_scratch(samples),
         compiler_params=pltpu.CompilerParams(
             collective_id=0, has_side_effects=True, vmem_limit_bytes=56 << 20
         ),
         name="step",
-    )(inv, unique_ids, next_ids, table, accum.reshape(rows_dev // 128, 128), *operands)
-
-
-PIECES = 4
-
-
-def finish_kernel(starts_ref, answers_ref, nt_ref, na_ref, out_ref, nt_out, na_out, answers, table, lines, sems):
-    some, size = answers.shape[0] // PIECES, table.shape[0] // PIECES
-
-    def fetch(k):
-        at = pl.ds(k * some, some)
-        return pltpu.make_async_copy(answers_ref.at[at], answers.at[at], sems.at[0, k])
-
-    def table_in(k):
-        at = pl.ds(k * size, size)
-        return pltpu.make_async_copy(nt_ref.at[at], table.at[at], sems.at[1, k])
-
-    def table_out(k):
-        at = pl.ds(k * size, size)
-        return pltpu.make_async_copy(table.at[at], nt_out.at[at], sems.at[2, k])
-
-    for k in range(PIECES):
-        fetch(k).start()
-    for k in range(PIECES):
-        table_in(k).start()
+    )(inverse, unique_ids, next_ids, table, accum.reshape(rows_dev // 128, 128), *operands)
+
+
+def finish_kernel(starts_ref, answers_ref, nt_ref, na_ref, out_ref, nt_out, na_out, lines, starts, sems):
+    scalars = pltpu.make_async_copy(starts_ref, starts, sems.at[2])
+    scalars.start()
+    table = pltpu.make_async_copy(nt_ref, nt_out, sems.at[0])
+    table.start()
     na_out[...] = na_ref[...]
+    scalars.wait()
 
     def place(k, carry):
-        for t in range(8):
-            o = k * 8 + t
-            lines[pl.ds(starts_ref[0, o], RCAP), :] = answers[o]
+        for t in range(16):
+            o = k * 16 + t
+            lines[pl.ds(starts[0, o], RCAP), :] = answers_ref[o]
         return carry
 
-    for k in range(PIECES):
-        fetch(k).wait()
-        lax.fori_loop(k * some // 8, (k + 1) * some // 8, place, 0)
-        if k:
-            table_in(k - 1).wait()
-            table_out(k - 1).start()
-    table_in(PIECES - 1).wait()
-    table_out(PIECES - 1).start()
-    result = pltpu.make_async_copy(lines.at[pl.ds(0, out_ref.shape[0])], out_ref, sems.at[3, 0])
+    lax.fori_loop(0, answers_ref.shape[0] // 16, place, 0)
+    result = pltpu.make_async_copy(lines.at[pl.ds(0, out_ref.shape[0])], out_ref, sems.at[1])
     result.start()
-    for k in range(PIECES):
-        table_out(k).wait()
+    table.wait()
     result.wait()
 
 
@@ -572,7 +557,7 @@
     width = answers.shape[2]
     return pl.pallas_call(
         finish_kernel,
-        in_specs=[pl.BlockSpec(memory_space=pltpu.SMEM), free, free, vmem],
+        in_specs=[vmem] * 4,
         out_specs=[free, free, vmem],
         out_shape=[
             jax.ShapeDtypeStruct((asked, width), F32),
@@ -580,12 +565,11 @@
             jax.ShapeDtypeStruct(new_accum.shape, F32),
         ],
         scratch_shapes=[
-            pltpu.VMEM(answers.shape, F32),
-            pltpu.VMEM(new_table.shape, F32),
             pltpu.VMEM((asked + RCAP, width), F32),
-            pltpu.SemaphoreType.DMA((4, PIECES)),
+            pltpu.SMEM(starts.shape, jnp.int32),
+            pltpu.SemaphoreType.DMA((3,)),
         ],
-        compiler_params=pltpu.CompilerParams(vmem_limit_bytes=60 << 20),
+        compiler_params=pltpu.CompilerParams(vmem_limit_bytes=8 << 20),
         name="finish",
     )(starts, answers, new_table, new_accum)
 

time: 104 us -> 99.5 us (0.957)
  Pallas kernels: 96 us -> 91.8 us
    pallas_call x1, Pallas kernels: 91.5 us -> 89.1 us  [step(): pl.pallas_call(step_kernel, in_specs=[vmem] * 3 + [pl.BlockSpec(memory_sp...]
    pallas_call x1, Pallas kernels: 4.47 us -> 2.73 us  [finish(): pl.pallas_call(finish_kernel, in_specs=[vmem] * 4, out_specs=[free, free,...]
    unnamed x11, local copies, waits for them, and re-layouts: 2.24 us -> 3.44 us
where the time goes in v6:
time: 99.5 us; the launch traced here: 99.2 us
  Pallas kernels  91.8 us (92%)
  local copies, waits for them, and re-layouts  4.71 us (5%)
    pallas_call x1, Pallas kernels, step(): pl.pallas_call(step_kernel, in_specs=[vmem] * 3 + [pl.BlockSpec(memory_sp...  89.1 us
    unnamed x11, local copies, waits for them, and re-layouts  3.44 us
    pallas_call x1, Pallas kernels, finish(): pl.pallas_call(finish_kernel, in_specs=[vmem] * 4, out_specs=[free, free,...  2.73 us

profile of v6, /device:TPU:1, one launch (start us, length us, event | category | flops | bytes accessed | tf_op | source)
XLA Modules:
  0.0 99.2 jit_solution(8688890014425029716)
XLA Ops:
  0.6 0.0 copy-start
  0.6 0.0 copy-start.1
  0.7 1.2 %copy-done = bf16[100,100,39]{1,2,0:T(8,128)(2,1)S(1)} copy-done((bf16[100,100,39]{1,2,0:T(8,128)(2,1)S(1)}, bf16[100,100,39]{1,2,0:T(8,128)(2,1)}, u32[]{:S(2)}) %copy-start) | copy-done | bytes 780024
  1.9 1.0 fusion
  2.8 1.2 %copy.23 = f32[32,100,39]{1,2,0:T(8,128)} copy(f32[32,100,39]{1,0,2:T(8,128)S(1)} %fusion) | data formatting | bytes 998400 | tf_op jit(solution)/shard_map/hij,nh->nji/dot_general | solution.py:187
  4.0 0.0 copy-done.1
  4.0 0.1 bitcast_add_fusion
  4.2 0.0 copy-start.2
  4.3 0.1 subtract_convert_fusion
  4.4 0.8 pad_maximum_fusion.w1b_ref
  5.2 0.4 copy-done.2
  5.6 1.8 %copy.17 = bf16[100,100,39]{0,1,2:T(8,128)(2,1)} copy(bf16[100,100,39]{1,2,0:T(8,128)(2,1)S(1)} %copy-done.2) | data formatting | bytes 1560000 | tf_op args[5]
  7.4 89.1 %step.1 = (f32[4096,128]{1,0:T(8,128)S(1)}, f32[32,128]{1,0:T(8,128)S(1)}, f32[256,8,128]{2,1,0:T(8,128)S(1)}, s32[8,256]{1,0:T(8,128)S(1)}) custom-call(s32[32,39]{1,0:T(8,128)} %inv_ref.1, s32[1,768]{1,0:T(1,128)} %ids_ref.1, s32[1,1536]{1,0:T(1,128)} %next_ref.1, f32[4096,128]{1,0:T(8,128)} %table_ref.1, f32[32,128]{1,0:T(8,128)} %bitcast.31, ...), custom_call_target="tpu_custom_call" | custom-call | tf_op jit(solution)/shard_map/step/pallas_call | solution.py:502
  96.5 2.7 %finish.1 = (f32[1536,128]{1,0:T(8,128)}, f32[4096,128]{1,0:T(8,128)}, f32[32,128]{1,0:T(8,128)}) custom-call(s32[8,256]{1,0:T(8,128)S(1)} %get-tuple-element.10.starts_ref, f32[256,8,128]{2,1,0:T(8,128)S(1)} %get-tuple-element.11.answers_ref, f32[4096,128]{1,0:T(8,128)S(1)} %get-tuple-element.12.nt_ref, f32[32,128]{1,0:T(8,128)S(1)} %get-tuple-element.13.na_ref), custom_call_target="tpu_custom_call" | custom-call | tf_op jit(solution)/shard_map/finish/pallas_call | solution.py:558
  (9 shorter events, 0.1 us)
Async XLA Ops:
  0.6 1.2 %copy-start = (bf16[100,100,39]{1,2,0:T(8,128)(2,1)S(1)}, bf16[100,100,39]{1,2,0:T(8,128)(2,1)}, u32[]{:S(2)}) copy-start(bf16[100,100,39]{1,2,0:T(8,128)(2,1)} %param.18) | copy-start | bytes 2340004
  0.6 3.4 %copy-start.1 = (bf16[100,39,39]{0,2,1:T(8,128)(2,1)S(1)}, bf16[100,39,39]{0,2,1:T(8,128)(2,1)}, u32[]{:S(2)}) copy-start(bf16[100,39,39]{0,2,1:T(8,128)(2,1)} %param.16) | copy-start | bytes 912604
  4.2 1.4 %copy-start.2 = (bf16[100,100,39]{1,2,0:T(8,128)(2,1)S(1)}, bf16[100,100,39]{1,2,0:T(8,128)(2,1)}, u32[]{:S(2)}) copy-start(bf16[100,100,39]{1,2,0:T(8,128)(2,1)} %param.17) | copy-start | bytes 2340004

commit v7 on v6

--- a/solution.py
+++ b/solution.py
@@ -37,14 +37,31 @@
     return slice(s * 128, (s + 1) * 128)
 
 
-def cin_layouts(e_ref, c1_ref, c2_ref, w1_ref, w2_ref, wide, columns, tops, w1t, w2b, w1f, w2f):
+def cin_layouts(e_ref, c1_ref, c2_ref, c3_ref, w1_ref, w2_ref, w3_ref, wide, columns, third, big, tops, w1t, w2b, w1f, w2f):
     fields, samples = e_ref.shape[0], e_ref.shape[1]
     maps = c1_ref.shape[1]
-    for ref in (columns, tops, w1t, w2b):
+    for ref in (columns, third, big, tops, w1t, w2b):
         ref[...] = jnp.zeros_like(ref)
+    third[:, :maps] = c3_ref[...]
     for f in range(fields):
         w1t[f * FP : f * FP + fields, :maps] = w1_ref[f]
-        w2b[f * HP : f * HP + maps, :maps] = w2_ref[f]
+
+    def widen(source):
+        def one(k, carry):
+            for t in range(10):
+                h = k * 10 + t
+                big[pl.ds(pl.multiple_of(h * FQ, 8), fields), :maps] = source[h].astype(F32)
+            return carry
+
+        lax.fori_loop(0, maps // 10, one, 0)
+
+    widen(w3_ref)
+    for f in range(fields):
+        filters = big[pl.ds(f, HP, stride=FQ), :].astype(BF)
+        tops[f * samples : (f + 1) * samples, :] = dot(third[:, :HP], filters)
+    widen(w2_ref)
+    for f in range(fields):
+        w2b[f * HP : (f + 1) * HP, :HP] = big[pl.ds(f, HP, stride=FQ), :].T[:HP].astype(BF)
     for f in range(fields):
         wide[f * samples : (f + 1) * samples, :] = e_ref[f].astype(F32)
     wide[fields * samples :, :] = jnp.zeros((wide.shape[0] - fields * samples, 128), F32)
@@ -57,10 +74,10 @@
             to[:, at] = source[at, :].astype(F32).T[:HP].astype(BF)
             return carry
 
-        lax.fori_loop(0, source.shape[0] // 128, turn, 0, unroll=5)
-
-
-def cin_first(g, top_ref, w2b_ref, wide, columns, tops, w1f, w2f, keep, p1, p2, l1f, mid, l2s, fill):
+        lax.fori_loop(0, source.shape[0] // 128, turn, 0, unroll=True)
+
+
+def cin_first(g, w2b_ref, wide, columns, tops, w1f, w2f, keep, p1, p2, l1f, mid, l2s, fill):
     ef, part, low, base = keep
     fields, samples = FIELDS, columns.shape[1]
     for s in range(2):
@@ -77,8 +94,7 @@
     next(fill, None)
     uppers = []
     for s in range(2):
-        tops[s, :fields, : top_ref.shape[2]] = top_ref[2 * g + s]
-        top, one = tops[s].T[:HP], e[:, half(s)]
+        top, one = tops[pl.ds(2 * g + s, FP, stride=samples), :].T[:HP], e[:, half(s)]
         hi, lo = halves(top)
         rest = (top - hi.astype(F32) - lo.astype(F32)).astype(BF)
         grad_two = dot(hi, one) + (dot(lo, one) + dot(rest, one))
@@ -105,7 +121,7 @@
             p2[j * HP : (j + 1) * HP, :] = (l3 * row16(j)[None]).reshape(HP, LANES)
         ready = (c + 1) * JC * HP
         if c + 1 < fields // JC:
-            ready = ready // 512 * 512
+            ready = ready // 1024 * 1024
         if ready > done:
             piece = dot(w2f[:, done:ready], p2[done:ready, :])
             if done:
@@ -126,7 +142,7 @@
     lower = (cots[:HQ] + lower).astype(F32)
     low[...] = jnp.concatenate([lower, jnp.zeros((KP - HQ, LANES), F32)], axis=0).astype(BF)
     for s in range(2):
-        hi, lo = halves(tops[s][:, :HP])
+        hi, lo = halves(tops[pl.ds(2 * g + s, FP, stride=samples), :][:, :HP])
         base[:, half(s)] = dot(hi, l2[:, half(s)]) + dot(lo, l2[:, half(s)])
 
 
@@ -158,11 +174,12 @@
 
 def cin_all(
     between,
-    e_ref, c1_ref, c2_ref, top_ref, w1_ref, w2_ref, w1b_ref, out_ref,
-    wide, columns, tops, w1t, w2b, w1f, w2f, p1, p2, l1f, mid, l2s, bot, *kept,
+    e_ref, c1_ref, c2_ref, c3_ref, w1_ref, w2_ref, w3_ref, w1b_ref, out_ref,
+    wide, columns, third, big, tops, w1t, w2b, w1f, w2f, p1, p2, l1f, mid, l2s, bot, *kept,
 ):
     keeps = (kept[:4], kept[4:])
-    cin_layouts(e_ref, c1_ref, c2_ref, w1_ref, w2_ref, wide, columns, tops, w1t, w2b, w1f, w2f)
+    cin_layouts(
+        e_ref, c1_ref, c2_ref, c3_ref, w1_ref, w2_ref, w3_ref, wide, columns, third, big, tops, w1t, w2b, w1f, w2f)
     turns = columns.shape[1] // 4
 
     def turn(t, carry):
@@ -171,7 +188,7 @@
             g = 2 * t + k
             fill = cin_last(jnp.maximum(g - 1, 0), w1b_ref, out_ref, keeps[1 - k], bot)
             cin_first(
-                g, top_ref, w2b, wide, columns, tops, w1f, w2f, keeps[k], p1, p2, l1f, mid, l2s, fill
+                g, w2b, wide, columns, tops, w1f, w2f, keeps[k], p1, p2, l1f, mid, l2s, fill
             )
         return carry
 
@@ -184,22 +201,23 @@
     maps, fields = w_first.shape[:2]
     e = jnp.transpose(embeddings, (1, 0, 2))
 
-    top = jnp.einsum("hij,nh->nji", w_third, cot_third, preferred_element_type=F32)
-    w2 = jnp.transpose(w_second, (2, 1, 0))
+    w2, w3 = jnp.transpose(w_second, (0, 2, 1)), jnp.transpose(w_third, (0, 2, 1))
     w1 = jnp.transpose(w_first, (1, 2, 0))
     both = w1.astype(F32)
     both = both + jnp.swapaxes(both, 0, 1)
     both = jnp.pad(both, ((0, FQ - fields), (0, FQ - fields), (0, KP - maps)))
     both = [both[8 * b : 8 * b + 8, : 8 * (b + 1)].reshape(-1, KP) for b in range(FQ // 8)]
     w1b = jnp.concatenate(halves(jnp.concatenate(both, axis=0)), axis=1)
-    return e, cot_first, cot_second, top, w1, w2, w1b
+    return e, cot_first, cot_second, cot_third, w1, w2, w3, w1b
 
 
 def cin_scratch(samples):
     return [
         pltpu.VMEM((FQ * samples, 128), F32),
         pltpu.VMEM((2 * HP, samples), BF),
-        pltpu.VMEM((2, FP, 128), F32),
+        pltpu.VMEM((samples, 128), BF),
+        pltpu.VMEM((HP * FQ, 128), F32),
+        pltpu.VMEM((FP * samples, 128), F32),
         pltpu.VMEM((FQ * FP, KP), BF),
         pltpu.VMEM((FQ * HP, KP), BF),
         pltpu.VMEM((HP, FQ * FP), BF),
@@ -327,13 +345,19 @@
 
 def step_kernel(
     inv_ref, ids_ref, next_ref, table_ref, accum_ref,
-    e_ref, c1_ref, c2_ref, top_ref, w1_ref, w2_ref, w1b_ref,
+    e_ref, c1_ref, c2_ref, c3_ref, w1_ref, w2_hbm, w3_hbm, w1b_ref,
     nt_ref, na_ref, answers_ref, starts_ref,
     hot, high, grad, grads, send, rows, found, ask_v, ask_s, rows_out, rows_in, answers_out, answers_in, own, table_in,
-    *scratch,
+    w2_ref, w3_ref, filters_in, *scratch,
 ):
     tree = Tree()
     tree.arrive()
+    filters = [
+        pltpu.make_async_copy(w3_hbm, w3_ref, filters_in.at[0]),
+        pltpu.make_async_copy(w2_hbm, w2_ref, filters_in.at[1]),
+    ]
+    for copy in filters:
+        copy.start()
     table_copy = pltpu.make_async_copy(table_ref, nt_ref, table_in)
     table_copy.start()
     grad[...] = jnp.zeros_like(grad)
@@ -364,8 +388,10 @@
         pl.when(turn == turns // 2)(tree.turn)
         pl.when(turn == turns * 3 // 4)(tree.release)
 
+    for copy in filters:
+        copy.wait()
     cin_all(
-        between, e_ref, c1_ref, c2_ref, top_ref, w1_ref, w2_ref, w1b_ref, grads, *scratch
+        between, e_ref, c1_ref, c2_ref, c3_ref, w1_ref, w2_ref, w3_ref, w1b_ref, grads, *scratch
     )
 
     g = jnp.concatenate(halves(grads[...].reshape(count, width)), axis=1)
@@ -498,10 +524,10 @@
     rows_dev, width = table.shape
     samples = inverse.shape[0]
     owners = lax.axis_size("group") * lax.axis_size("member")
-    vmem = pl.BlockSpec(memory_space=pltpu.VMEM)
+    vmem, free = pl.BlockSpec(memory_space=pltpu.VMEM), pl.BlockSpec(memory_space=pl.ANY)
     return pl.pallas_call(
         step_kernel,
-        in_specs=[vmem] * 3 + [pl.BlockSpec(memory_space=pl.ANY)] + [vmem] * (1 + len(operands)),
+        in_specs=[vmem] * 3 + [free] + [vmem] * 6 + [free] * 2 + [vmem],
         out_specs=[vmem, vmem, vmem, vmem],
         out_shape=[
             pltpu.VMEM(table.shape, F32),
@@ -523,6 +549,8 @@
             pltpu.SemaphoreType.DMA((CLASSES,)),
         ]
         + [pltpu.SemaphoreType.DMA] * 4
+        + [pltpu.VMEM(w.shape, BF) for w in operands[5:7]]
+        + [pltpu.SemaphoreType.DMA((2,))]
         + cin_scratch(samples),
         compiler_params=pltpu.CompilerParams(
             collective_id=0, has_side_effects=True, vmem_limit_bytes=56 << 20

time: 99.5 us -> 96.7 us (0.972)
  local copies, waits for them, and re-layouts: 4.71 us -> 0.09 us
  Pallas kernels: 91.8 us -> 93.7 us
  other arithmetic: 0.96 us -> 2.08 us
    unnamed x11 -> x4, local copies, waits for them, and re-layouts: 3.44 us -> 0.03 us
    pallas_call x1, Pallas kernels: 89.1 us -> 91 us  [step(): pl.pallas_call(step_kernel, in_specs=[vmem] * 3 + [free] + [vmem] * 6 + [...]
    dot_general x1 -> x0, local copies, waits for them, and re-layouts: 1.21 us -> none  [cin_operands(): jnp.einsum('hij,nh->nji', w_third, cot_third, preferred_element_type=F32)]
    add x1, other arithmetic: 0.06 us -> 1.18 us  [cin_operands(): both = both + jnp.swapaxes(both, 0, 1)]
where the time goes in v7:
time: 96.7 us; the launch traced here: 96.6 us
  Pallas kernels  93.7 us (97%)
  other arithmetic  2.08 us (2%)
    pallas_call x1, Pallas kernels, step(): pl.pallas_call(step_kernel, in_specs=[vmem] * 3 + [free] + [vmem] * 6 + [...  91 us
    pallas_call x1, Pallas kernels, finish(): pl.pallas_call(finish_kernel, in_specs=[vmem] * 4, out_specs=[free, free,...  2.73 us

profile of v7, /device:TPU:1, one launch (start us, length us, event | category | flops | bytes accessed | tf_op | source)
XLA Modules:
  0.0 96.6 jit_solution(15773846389410758739)
XLA Ops:
  0.6 1.2 %bitcast_add_fusion = f32[39,39,100]{2,1,0:T(8,128)S(1)} fusion(bf16[100,39,39]{0,2,1:T(8,128)(2,1)} %param.16), kind=kLoop, calls=%fused_computation | loop fusion | flops 456300 | bytes 912600 | tf_op jit(solution)/shard_map/add | solution.py:207
  2.0 0.1 subtract_convert_fusion
  2.0 0.8 pad_maximum_fusion.w1b_ref
  2.9 91.0 %step.1 = (f32[4096,128]{1,0:T(8,128)S(1)}, f32[32,128]{1,0:T(8,128)S(1)}, f32[256,8,128]{2,1,0:T(8,128)S(1)}, s32[8,256]{1,0:T(8,128)S(1)}) custom-call(s32[32,39]{1,0:T(8,128)} %inv_ref.1, s32[1,768]{1,0:T(1,128)} %ids_ref.1, s32[1,1536]{1,0:T(1,128)} %next_ref.1, f32[4096,128]{1,0:T(8,128)} %table_ref.1, f32[32,128]{1,0:T(8,128)} %bitcast.26, ...), custom_call_target="tpu_custom_call" | custom-call | tf_op jit(solution)/shard_map/step/pallas_call | solution.py:528
  93.9 2.7 %finish.1 = (f32[1536,128]{1,0:T(8,128)}, f32[4096,128]{1,0:T(8,128)}, f32[32,128]{1,0:T(8,128)}) custom-call(s32[8,256]{1,0:T(8,128)S(1)} %get-tuple-element.10.starts_ref, f32[256,8,128]{2,1,0:T(8,128)S(1)} %get-tuple-element.11.answers_ref, f32[4096,128]{1,0:T(8,128)S(1)} %get-tuple-element.12.nt_ref, f32[32,128]{1,0:T(8,128)S(1)} %get-tuple-element.13.na_ref), custom_call_target="tpu_custom_call" | custom-call | tf_op jit(solution)/shard_map/finish/pallas_call | solution.py:586
  (9 shorter events, 0.1 us)
